TPU v7x, 32 devices: a whole 2x2x4 slice. The times are simulated.
32 devices in a mesh: row: 4 (over x, core), col: 8 (over z, y).
Axes of the slice: x: 2, y: 2, z: 4, core: 2. Of those that a mesh axis runs over, the one named last changes fastest.
Arguments:
- adj_trailing: bfloat16 [4096, 8192], P('row', 'col'), may hold values from -6 to 6
- panel_rows0: bfloat16 [4096, 512], P('row'), may hold values from -0.09375 to 0.09375
- panel_rows1: bfloat16 [4096, 512], P('row'), may hold values from -0.09375 to 0.09375
- panel_cols0: bfloat16 [8192, 512], P('col'), may hold values from -0.0625 to 0.0625
- panel_cols1: bfloat16 [8192, 512], P('col'), may hold values from -0.0625 to 0.0625
- inv_diag0: float32 [512, 512], replicated, as said below
- inv_diag1: float32 [512, 512], replicated, as said below
- cross_block: float32 [512, 512], replicated, may hold values from -0.25 to 0.25
- panel_adj0: bfloat16 [4096, 512], P(('row', 'col')), may hold values from -6 to 6
- panel_adj1: bfloat16 [4096, 512], P(('row', 'col')), may hold values from -6 to 6
Outputs:
- row_adj1: float32 [4096, 512], P(('row', 'col'))
- row_adj0: float32 [4096, 512], P(('row', 'col'))
- col_adj1: float32 [8192, 512], P('col')
- col_adj0: float32 [8192, 512], P('col')
- diag_adj1: float32 [512, 512], replicated
- diag_adj0: float32 [512, 512], replicated
Inputs may be any that keep to these rules, and one draw needn't show every extreme that they name: `inv_diag0`: lower triangular, with diagonal entries of 1 to 2. `inv_diag1`: lower triangular, with diagonal entries of 1 to 2.
All inputs are finite; a program needn't handle non-finite values.
Results may differ from a plain program's by a relative error of at most 0.0003.
Values sent between devices are 32-bit elements; how exact they have to be, the bound alone decides.
No kernel may reach another device: no remote copies, remote signals or barrier semaphores. Data moves between devices by JAX's collectives and lax.ppermute only.
A program may use at most 128 MiB of HBM per device.

v0:
```python
import jax
import jax.numpy as jnp
from jax import lax
from jax.sharding import PartitionSpec as P


def trailing_term(adj_trailing, columns):
    return jnp.dot(adj_trailing, columns, preferred_element_type=jnp.float32)


def column_term(adj_trailing, rows):
    return -jnp.einsum("rc,rb->cb", adj_trailing, rows, preferred_element_type=jnp.float32)


def local(
    adj_trailing,
    panel_rows0,
    panel_rows1,
    panel_cols0,
    panel_cols1,
    inv_diag0,
    inv_diag1,
    cross_block,
    panel_adj0,
    panel_adj1,
):
    highest = lax.Precision.HIGHEST
    share = panel_adj1.shape[0]
    width = panel_cols1.shape[1]
    offset = lax.axis_index("col") * share
    own_rows1 = lax.dynamic_slice_in_dim(panel_rows1, offset, share, 0).astype(jnp.float32)
    own_rows0 = lax.dynamic_slice_in_dim(panel_rows0, offset, share, 0).astype(jnp.float32)
    both_cols = jnp.concatenate((panel_cols1, panel_cols0), axis=1)
    trail = lax.psum_scatter(
        trailing_term(adj_trailing, both_cols), "col", scatter_dimension=0, tiled=True
    )
    trail1 = trail[:, :width]
    trail0 = trail[:, width:]
    both_rows = jnp.concatenate((panel_rows1, panel_rows0), axis=1)
    column_sum = lax.psum(column_term(adj_trailing, both_rows), "row")
    col_adj1 = column_sum[:, :width]
    col_adj0 = column_sum[:, width:]
    bar1 = panel_adj1.astype(jnp.float32) - trail1
    row_adj1 = jnp.dot(bar1, inv_diag1, precision=highest)
    bar0 = (
        panel_adj0.astype(jnp.float32) - trail0 - jnp.dot(row_adj1, cross_block, precision=highest)
    )
    row_adj0 = jnp.dot(bar0, inv_diag0, precision=highest)
    gram1 = jnp.dot(bar1.T, own_rows1, precision=highest)
    gram0 = jnp.dot(bar0.T, own_rows0, precision=highest)
    local1 = jnp.dot(inv_diag1.T, gram1, precision=highest)
    local0 = jnp.dot(inv_diag0.T, gram0, precision=highest)
    summed1, summed0 = lax.psum((local1, local0), ("row", "col"))
    diag_adj1 = -jnp.tril(summed1)
    diag_adj0 = -jnp.tril(summed0)
    return (row_adj1, row_adj0, col_adj1, col_adj0, diag_adj1, diag_adj0)


def solution(mesh):
    return jax.shard_map(
        local,
        mesh=mesh,
        in_specs=(
            P("row", "col"),
            P("row", None),
            P("row", None),
            P("col", None),
            P("col", None),
            P(),
            P(),
            P(),
            P(("row", "col"), None),
            P(("row", "col"), None),
        ),
        out_specs=(
            P(("row", "col"), None),
            P(("row", "col"), None),
            P("col", None),
            P("col", None),
            P(),
            P(),
        ),
        check_vma=False,
    )
```

profile of v0, /device:TPU:0, one launch (start us, length us, event | category | flops | bytes accessed | tf_op | source)
XLA Modules:
  0.0 268.3 jit_solution(9926880069097998248)
XLA Ops:
  8.0 0.0 copy-start
  8.0 0.0 reduce-scatter.2.cloned.1.call-start
  8.1 1.5 copy-done
  9.6 5.9 %convolution_bitcast_fusion = f32[1024,1024]{0,1:T(8,128)} fusion(bf16[1024,1024]{1,0:T(8,128)(2,1)S(1)} %copy-done, bf16[1024,512]{1,0:T(8,128)(2,1)} %param.13, bf16[1024,512]{1,0:T(8,128)(2,1)} %param.14), kind=kOutput, calls=%fused_computation.1 | convolution fusion | flops 2151677952 | bytes 8388608 | tf_op jit(solution)/shard_map/dot_general | solution.py:8
  15.5 0.0 copy-start.9
  15.5 0.0 reduce-scatter.2.cloned.1.call-update
  15.5 0.0 all-reduce.4.cloned.1.call-start
  15.6 1.1 copy-done.9
  16.7 5.6 %negate_bitcast_fusion = f32[1024,1024]{0,1:T(8,128)} fusion(bf16[1024,1024]{1,0:T(8,128)(2,1)S(1)} %copy-done, bf16[1024,512]{1,0:T(8,128)(2,1)} %param.11, bf16[1024,512]{1,0:T(8,128)(2,1)S(1)} %copy-done.9), kind=kOutput, calls=%fused_computation | convolution fusion | flops 2152726528 | bytes 8388608 | tf_op jit(solution)/shard_map/rc,rb->cb/dot_general | solution.py:12
  22.3 0.0 copy-start.7
  22.3 0.0 copy-start.8
  22.3 0.0 copy-start.2
  22.3 0.0 all-reduce.4.cloned.1.call-update
  22.3 0.2 all-reduce.6.cloned.1.call-start
  22.5 0.6 copy-done.7
  23.2 0.1 copy.16
  23.3 0.0 copy-done.8
  23.3 0.8 copy.17
  24.1 83.0 %reduce-scatter.2.cloned.1.call-done = f32[128,1024]{0,1:T(8,128)} async-done(((f32[1024,1024]{0,1:T(8,128)}), f32[128,1024]{0,1:T(8,128)}) %reduce-scatter.2.cloned.1.call-update) | async-done | bytes 524304 | tf_op jit(solution)/shard_map/reduce_scatter | solution.py:34
  107.1 0.0 copy-done.2
  107.1 0.0 copy-start.6
  107.1 1.8 fusion.7
  108.9 0.0 copy-done.6
  108.9 0.0 copy-start.5
  108.9 0.0 copy-start.4
  108.9 0.0 copy-start.3
  108.9 2.9 %convolution_subtract_fusion = f32[128,512]{0,1:T(8,128)S(1)} fusion(f32[128,512]{1,0:T(8,128)S(1)} %fusion.7, f32[512,512]{1,0:T(8,128)S(1)} %copy-done.6, f32[128,1024]{0,1:T(8,128)} %reduce-scatter.2.cloned.1.call-done, bf16[128,512]{0,1:T(8,128)(2,1)} %copy.17), kind=kOutput, calls=%fused_computation.10 | convolution fusion | flops 402849792 | bytes 1966080 | tf_op jit(solution)/shard_map/dot_general | solution.py:46
  111.8 0.0 copy-done.5
  111.8 1.5 fusion.8
  113.3 0.0 copy-done.4
  113.3 0.0 copy-start.1
  113.3 1.6 fusion.6
  114.9 0.0 copy-done.3
  114.9 2.8 %convolution_bitcast_fusion.2 = f32[512,512]{0,1:T(8,128)} fusion(f32[512,512]{1,0:T(8,128)S(1)} %fusion.6, f32[512,512]{1,0:T(8,128)S(1)} %copy-done.3), kind=kOutput, calls=%fused_computation.9 | convolution fusion | flops 1610612736 | bytes 3145728 | tf_op jit(solution)/shard_map/dot_general | solution.py:51
  117.8 0.0 copy-done.1
  117.8 2.8 %convolution_bitcast_fusion.1 = f32[512,512]{0,1:T(8,128)} fusion(f32[512,512]{1,0:T(8,128)S(1)} %fusion.8, f32[512,512]{1,0:T(8,128)S(1)} %copy-done.1), kind=kOutput, calls=%fused_computation.8 | convolution fusion | flops 1610612736 | bytes 3145728 | tf_op jit(solution)/shard_map/dot_general | solution.py:52
  120.6 0.0 all-reduce.6.cloned.1.call-update
  120.6 0.0 all-reduce.4.cloned.1.call-done
  120.6 4.8 %fusion.15 = (f32[1024,512]{0,1:T(8,128)}, f32[1024,512]{0,1:T(8,128)}) fusion(f32[1024,1024]{0,1:T(8,128)} %all-reduce.4.cloned.1.call-done), kind=kLoop, calls=%fused_computation.25 | loop fusion | bytes 8388608 | tf_op jit(solution)/shard_map/slice | solution.py:42
  125.5 2.9 %copy.19 = f32[1024,512]{1,0:T(8,128)} copy(f32[1024,512]{0,1:T(8,128)} %get-tuple-element.15) | data formatting | bytes 4194304
  128.4 2.9 %copy.20 = f32[1024,512]{1,0:T(8,128)} copy(f32[1024,512]{0,1:T(8,128)} %get-tuple-element.14) | data formatting | bytes 4194304
  131.3 1.5 fusion.16
  132.7 121.5 %all-reduce.6.cloned.1.call-done = (f32[512,512]{0,1:T(8,128)}, f32[512,512]{0,1:T(8,128)}) async-done(((f32[512,512]{0,1:T(8,128)}, f32[512,512]{0,1:T(8,128)}), (f32[512,512]{0,1:T(8,128)}, f32[512,512]{0,1:T(8,128)})) %all-reduce.6.cloned.1.call-update) | async-done | bytes 2097168 | tf_op jit(solution)/shard_map/psum | solution.py:53
  254.2 2.8 %select_negate_fusion = (f32[512,512]{0,1:T(8,128)S(1)}, f32[512,512]{0,1:T(8,128)}) fusion(f32[512,512]{0,1:T(8,128)} %get-tuple-element.13, f32[512,512]{0,1:T(8,128)} %get-tuple-element.12), kind=kLoop, calls=%fused_computation.11 | loop fusion | flops 1310720 | bytes 4194304 | tf_op jit(solution)/shard_map/neg | solution.py:55
  257.0 2.5 copy.21
  259.6 1.3 copy.22
Async XLA Ops:
  8.0 1.6 copy-start
  8.0 99.0 %reduce-scatter.2.cloned.1.call-start = ((), (), s32[]{:S(2)}) async-start(), calls=%async_computation.1 | async-start | bytes 4718592 | tf_op jit(solution)/shard_map/reduce_scatter | solution.py:34
  15.5 1.2 copy-start.9
  15.5 105.1 %all-reduce.4.cloned.1.call-start = ((), (), s32[]{:S(2)}) async-start(), calls=%async_computation.2 | async-start | bytes 8388608 | tf_op jit(solution)/shard_map/psum | solution.py:40
  22.3 0.9 copy-start.7
  22.3 1.0 copy-start.8
  22.3 84.8 %copy-start.2 = (f32[512,512]{1,0:T(8,128)S(1)}, f32[512,512]{1,0:T(8,128)}, u32[]{:S(2)}) copy-start(f32[512,512]{1,0:T(8,128)} %param.16) | copy-start | bytes 3145732
  22.3 231.9 %all-reduce.6.cloned.1.call-start = ((), (), s32[]{:S(2)}) async-start(), calls=%async_computation.3 | async-start | bytes 4194304 | tf_op jit(solution)/shard_map/psum | solution.py:53
  107.1 1.8 copy-start.6
  108.9 3.0 %copy-start.5 = (f32[128,512]{1,0:T(8,128)}, f32[128,512]{1,0:T(8,128)S(1)}, u32[]{:S(2)}) copy-start(f32[128,512]{1,0:T(8,128)S(1)} %fusion.7) | copy-start | bytes 786436
  108.9 4.4 %copy-start.4 = (f32[128,1024]{0,1:T(8,128)S(1)}, f32[128,1024]{0,1:T(8,128)}, u32[]{:S(2)}) copy-start(f32[128,1024]{0,1:T(8,128)} %reduce-scatter.2.cloned.1.call-done) | copy-start | bytes 1572868
  108.9 6.0 %copy-start.3 = (f32[512,512]{1,0:T(8,128)S(1)}, f32[512,512]{1,0:T(8,128)}, u32[]{:S(2)}) copy-start(f32[512,512]{1,0:T(8,128)} %param.16) | copy-start | bytes 3145732
  113.3 4.4 %copy-start.1 = (f32[512,512]{1,0:T(8,128)S(1)}, f32[512,512]{1,0:T(8,128)}, u32[]{:S(2)}) copy-start(f32[512,512]{1,0:T(8,128)} %param.15) | copy-start | bytes 3145732
Sparse Core Ops, SparseCore 0:
  15.6 91.3 reduce-scatter.1
Sparse Core Ops, SparseCore 1:
  22.4 88.0 all-reduce.3
  120.7 133.5 all-reduce.5
where the time goes:
time: 269 us; the launch traced here: 268 us
  waiting for transfers between devices  205 us (76%)
  matrix products  26.3 us (10%)
  local copies, waits for them, and re-layouts  18.7 us (7%)
  between operations  15.6 us (6%)
  other arithmetic  2.78 us (1%)
    psum x1, waiting for transfers between devices, local(): summed1, summed0 = lax.psum((local1, local0), ('row', 'col'))  122 us
    reduce_scatter x1, waiting for transfers between devices, local(): lax.psum_scatter(trailing_term(adj_trailing, both_cols), 'col', scatter_d...  83 us
    unnamed x26, local copies, waits for them, and re-layouts  13.9 us
    dot_general x1, matrix products, trailing_term(): return jnp.dot(adj_trailing, columns, preferred_element_type=jnp.float32)  5.88 us
    dot_general x1, matrix products, column_term(): jnp.einsum('rc,rb->cb', adj_trailing, rows, preferred_element_type=jnp.fl...  5.57 us
  transfers between devices with their start and end apart: 3, of which 2 were waited for; matrix products, arithmetic and copies ran while one was open for 12% of the time, Pallas kernels for 0%

commit v1 on v0

v1 whole, which is shorter than its diff:
```python
import functools

import jax
import jax.numpy as jnp
from jax import lax
from jax.experimental import pallas as pl
from jax.experimental.pallas import tpu as pltpu
from jax.sharding import PartitionSpec as P

F32 = jnp.float32
BF16 = jnp.bfloat16
LANES = 128

T_SHARES = ((1, 0, 4), (1, 4, 4), (0, 0, 4), (0, 4, 4))
C_SHARES = ((0, 2), (2, 4), (6, 2))


def mm(a, b):
    return jnp.dot(a, b, preferred_element_type=F32)


def mm_t(a, b):
    return lax.dot_general(a, b, (((0,), (0,)), ((), ())), preferred_element_type=F32)


def split2(x):
    hi = x.astype(BF16)
    return hi, (x - hi.astype(F32)).astype(BF16)


def split3(x):
    hi = x.astype(BF16)
    rest = x - hi.astype(F32)
    mid = rest.astype(BF16)
    return hi, mid, (rest - mid.astype(F32)).astype(BF16)


def mm3(a, b):
    ah, al = split2(a)
    bh, bl = split2(b)
    return mm(ah, bh) + (mm(ah, bl) + mm(al, bh))


SMEM = pl.BlockSpec(memory_space=pltpu.SMEM)
VMEM = pl.BlockSpec(memory_space=pltpu.VMEM)
ANY = pl.BlockSpec(memory_space=pl.ANY)


def f32(*shape):
    return jax.ShapeDtypeStruct(shape, F32)


def kernel(body, scalars, args, outs, flops=0, specs=None, out_specs=None, **more):
    specs = [VMEM] * len(args) if specs is None else specs
    out_specs = [VMEM] * len(outs) if out_specs is None else out_specs
    size = sum(a.size * a.dtype.itemsize for a in args)
    return pl.pallas_call(
        body,
        in_specs=[SMEM] + specs,
        out_specs=out_specs,
        out_shape=outs,
        cost_estimate=pl.CostEstimate(
            flops=int(flops), bytes_accessed=int(size), transcendentals=0
        ),
        compiler_params=pltpu.CompilerParams(vmem_limit_bytes=16 * 2**20),
        **more,
    )(scalars, *args)


CORE, PAIR, BIT = 0, 1, 2


def rows_of(ref, parity, blk):
    pairs = ref.shape[0] // (2 * blk)
    return jnp.concatenate(
        [ref[pl.ds(pl.multiple_of((2 * i + parity) * blk, blk), blk), :] for i in range(pairs)],
        axis=0,
    )


def trail_block(a, c_ref, start, o_ref):
    o_ref[...] = mm(a, c_ref[:, start : start + o_ref.shape[1]])


def column_block(at, r1_ref, r0_ref, o_ref):
    b = r1_ref.shape[1]
    o_ref[:, :b] = -mm_t(at, r1_ref[...])
    o_ref[:, b:] = -mm_t(at, r0_ref[...])


def window_cols(ref, start, side, half):
    return ref[:, pl.ds(pl.multiple_of(start + side * half, LANES), half)]


def trail_body(blk, plan, s, a_hbm, c1_hbm, c0_hbm, *refs):
    o_refs, (a_ref, c1_ref, c0_ref, sem) = refs[:-4], refs[-4:]
    pairs = a_ref.shape[1] // blk
    depth = c1_ref.shape[0] // 2
    loads = {0: [], 1: [], "c1": [], "c0": []}
    count = 0

    def load(key, src, dst):
        nonlocal count
        loads[key].append(pltpu.make_async_copy(src, dst, sem.at[count]))
        loads[key][-1].start()
        count += 1

    def load_rows(own):
        parity = s[BIT] if own else 1 - s[BIT]
        for i in range(pairs):
            at = pl.multiple_of((2 * i + parity) * blk, blk)
            load(own, a_hbm.at[pl.ds(at, blk)], a_ref.at[own, pl.ds(i * blk, blk)])

    def load_cols(key, src, dst):
        for i in range(2):
            at = pl.ds(i * depth, depth)
            load(key, src.at[at], dst.at[at])

    load_rows(0)
    load_cols("c1", c1_hbm, c1_ref)
    load_cols("c0", c0_hbm, c0_ref)
    load_rows(1)
    for (own, panel, start), o_ref in zip(plan, o_refs):
        for key in (own, "c1" if panel else "c0"):
            for c in loads[key]:
                c.wait()
            loads[key] = []
        trail_block(a_ref[own], c1_ref if panel else c0_ref, start, o_ref)


def column_body(sides, plan, s, a_ref, r1_ref, r0_ref, *o_refs):
    for own, o_ref in zip(sides, o_refs):
        side = s[CORE] if own else 1 - s[CORE]
        at = [window_cols(a_ref, start, side, half) for start, half in plan]
        column_block(jnp.concatenate(at, axis=1), r1_ref, r0_ref, o_ref)


def write_body(starts, s, *refs):
    n = len(starts)
    d1_ref, d0_ref, sem = refs[-3:]
    copies = []
    for k, start in enumerate(starts):
        for ref, side in ((refs[k], s[CORE]), (refs[n + k], 1 - s[CORE])):
            half, b = ref.shape[0], ref.shape[1] // 2
            at = pl.ds(pl.multiple_of(start + side * half, 8), half)
            for lanes, out in ((slice(0, b), d1_ref), (slice(b, 2 * b), d0_ref)):
                copies.append(
                    pltpu.make_async_copy(ref.at[:, lanes], out.at[at], sem.at[len(copies)])
                )
    for c in copies:
        c.start()
    for c in copies:
        c.wait()


def iotas(b):
    return (
        lax.broadcasted_iota(jnp.int32, (b, b), 0),
        lax.broadcasted_iota(jnp.int32, (b, b), 1),
    )


def diag_body(blk, n1, s, r1_ref, r0_ref, p1_ref, p0_ref, inv1_ref, inv0_ref, cross_ref, *refs):
    keep_ref, send_ref, g1, g10, g0, buf = refs[-6:]
    t_refs = refs[:-6]
    nt = len(t_refs) // 2
    b = inv1_ref.shape[0]
    h = b // 2
    for own in (0, 1):
        parity = s[BIT] if own else 1 - s[BIT]
        r1, r0 = rows_of(r1_ref, parity, blk), rows_of(r0_ref, parity, blk)
        n = r0.shape[0]
        place = lax.broadcasted_iota(jnp.int32, (n, 1), 0) // blk == s[PAIR]
        ts = t_refs[own * nt : (own + 1) * nt]
        for panel in (1, 0):
            mine = ts[:n1] if panel else ts[n1:]
            bar = -jnp.concatenate([t[...] for t in mine], axis=1)
            if own:
                p = (p1_ref if panel else p0_ref)[...].astype(F32)
                bar = bar + jnp.where(place, jnp.concatenate([p] * (n // blk), axis=0), 0.0)
            for side in (0, 1):
                at = slice(side * h, (side + 1) * h)
                parts = jnp.concatenate(split3(bar[:, at]), axis=1)
                top = b if side else h
                todo = [(g1, r1[:, :top]), (g10, r0)] if panel else [(g0, r0[:, :top])]
                for g, r in todo:
                    x = mm_t(r, parts)
                    x = x[:, :h] + (x[:, h : 2 * h] + x[:, 2 * h :])
                    k = r.shape[1]
                    if own:
                        x = x + g[:k, at]
                    g[:k, at] = x
    x10 = g10[...]
    left = mm3(x10, inv1_ref[:, :h])
    right = mm3(x10[:, h:], inv1_ref[h:, h:])
    x10 = jnp.concatenate([left, right], axis=1)
    g0[:h, :h] = g0[:h, :h] - mm3(x10[:h], cross_ref[:, :h])
    g0[:, h:] = g0[:, h:] - mm3(x10, cross_ref[:, h:])
    i, j = iotas(b)
    low = jnp.zeros((h, h), F32)

    def upper(g, inv_ref):
        left = mm3(g[:h, :], inv_ref[:, :h])
        right = mm3(g[:, h:], inv_ref[h:, h:])
        return jnp.concatenate([jnp.concatenate([left, low], axis=0), right], axis=1)

    l0 = upper(g0, inv0_ref)
    both = jnp.where(i <= j, upper(g1, inv1_ref), l0.T)
    diag = jnp.sum(jnp.where(i == j, l0, 0.0), axis=0, keepdims=True)
    k = b // LANES
    for p in range(k):
        buf[p * b : (p + 1) * b, :] = both[:, p * LANES : (p + 1) * LANES]
    buf[k * b :, :] = jnp.zeros((buf.shape[0] - k * b, LANES), F32)
    for p in range(k):
        buf[k * b + p : k * b + p + 1, :] = diag[:, p * LANES : (p + 1) * LANES]
    half = buf.shape[0] // 2
    core = s[CORE]
    keep_ref[...] = buf[pl.ds(pl.multiple_of(core * half, 8), half), :]
    send_ref[...] = buf[pl.ds(pl.multiple_of((1 - core) * half, 8), half), :]


def unpack_body(s, m_ref, t_ref, d1_ref, d0_ref, buf):
    half = m_ref.shape[0]
    core = s[CORE]
    buf[pl.ds(pl.multiple_of(core * half, 8), half), :] = m_ref[...]
    buf[pl.ds(pl.multiple_of((1 - core) * half, 8), half), :] = t_ref[...]
    b = d1_ref.shape[0]
    k = b // LANES
    m = jnp.concatenate([buf[p * b : (p + 1) * b, :] for p in range(k)], axis=1)
    diag = jnp.concatenate([buf[k * b + p : k * b + p + 1, :] for p in range(k)], axis=1)
    i, j = iotas(b)
    d1_ref[...] = -jnp.where(i <= j, m, 0.0).T
    d0_ref[...] = -jnp.where(i > j, m, jnp.where(i == j, diag, 0.0))


def gather_sums(refs):
    return jnp.concatenate([a[...] + b[...] for a, b in zip(refs[::2], refs[1::2])], axis=1)


def row1_body(s, p1_ref, p0_ref, inv1_ref, cross_ref, *refs):
    row1_ref, q_ref = refs[-2:]
    bar1 = p1_ref[...].astype(F32) - gather_sums(refs[:-2])
    row1 = mm3(bar1, inv1_ref[...])
    row1_ref[...] = row1
    q_ref[...] = p0_ref[...].astype(F32) - mm3(row1, cross_ref[...])


def row0_body(s, q_ref, inv0_ref, *refs):
    bar0 = q_ref[...] - gather_sums(refs[:-1])
    refs[-1][...] = mm3(bar0, inv0_ref[...])


def make_local(n_row, n_col):
    col_bits = n_col.bit_length() - 1
    row_bits = n_row.bit_length() - 1

    def swap(axis, a, bit):
        size = n_row if axis == "row" else n_col
        return lax.ppermute(a, axis, [(i, i ^ (1 << bit)) for i in range(size)])

    def body(adj, rows0, rows1, cols0, cols1, inv0, inv1, cross, p0, p1):
        rows, b = rows1.shape
        blk = p1.shape[0]
        window = adj.shape[1]
        me_row = lax.axis_index("row")
        me_col = lax.axis_index("col")
        bits = [(me_col >> k) % 2 for k in range(col_bits)]
        s = jnp.stack([me_row % 2, me_col // 2] + bits).astype(jnp.int32)
        sides = {("col", k): bit for k, bit in enumerate(bits)}
        sides |= {("row", k): (me_row >> k) % 2 for k in range(row_bits)}
        sides = {key: side.astype(jnp.uint32) for key, side in sides.items()}
        values = lax.optimization_barrier(
            (s, [(x, 1 - x, x == 0) for x in sides.values()])
        )
        s, sides = values[0], dict(zip(sides, values[1]))

        def pick(x, index):
            zero = jnp.uint32(0)
            shape = (x.shape[0], 1) + x.shape[2:]
            return lax.dynamic_slice(x, (zero, index, zero, zero), shape)

        def add(x, y):
            return x + y

        def add_split(x, y, key, split):
            x = add(x, y)
            n, w = x.shape
            x = x.reshape(n // (2 * split), 2, split, w)
            return tuple(
                pick(x, side).reshape(n // 2, w) for side in sides[key][:2]
            )

        def ordered(key, m, other):
            low = sides[key][2]
            return jnp.concatenate(
                [jnp.where(low, m, other), jnp.where(low, other, m)], axis=0
            )

        half_rows = rows // 2
        shares = [(p, st * b // 8, w * b // 8) for p, st, w in T_SHARES]
        windows = [(st * window // 8, w * window // 16) for st, w in C_SHARES]

        nt = len(shares)
        plan = [(own, p, st) for own in (0, 1) for p, st, _ in shares]
        out = kernel(
            functools.partial(trail_body, blk, plan),
            s,
            [adj, cols1, cols0],
            [f32(half_rows, w) for _, _, w in shares + shares],
            4 * rows * window * b,
            specs=[pl.BlockSpec(memory_space=pltpu.HBM)] * 3,
            scratch_shapes=[
                pltpu.VMEM((2, half_rows, window), adj.dtype),
                pltpu.VMEM((window, b), cols1.dtype),
                pltpu.VMEM((window, b), cols0.dtype),
                pltpu.SemaphoreType.DMA((n_col + 4,)),
            ],
        )
        t_other, t_own = list(out[:nt]), list(out[nt:])
        t_recv = [swap("col", t, 0) for t in t_other]

        def columns(sides, some):
            width = sum(w for _, w in some)
            return kernel(
                functools.partial(column_body, sides, some),
                s,
                [adj, rows1, rows0],
                [f32(width, 2 * b)] * len(sides),
                len(sides) * 4 * rows * width * b,
            )

        (c_other,) = columns((0,), windows[:1])
        c_recv = swap("row", c_other, 0)
        (c_own,) = columns((1,), windows[:1])
        sums = [add(c_own, c_recv)]
        c_other, c_own = columns((0, 1), windows[1:])
        c_recv = swap("row", c_other, 0)
        at = 0
        for _, w in windows[1:]:
            sums.append(c_own[at : at + w] + c_recv[at : at + w])
            at += w

        held, theirs = [], []
        for total in sums:
            for bit in range(1, row_bits):
                total = add(total, swap("row", total, bit))
            held.append(total)
            theirs.append(swap("row", total, 0))
        outs = []
        for ks in (range(len(sums) - 1), range(len(sums) - 1, len(sums))):
            args = [held[k] for k in ks] + [theirs[k] for k in ks]
            n = len(args)
            outs = list(
                kernel(
                    functools.partial(write_body, [windows[k][0] for k in ks]),
                    s,
                    args + outs,
                    [f32(window, b)] * 2,
                    specs=[VMEM] * n + [ANY] * len(outs),
                    out_specs=[ANY, ANY],
                    scratch_shapes=[pltpu.SemaphoreType.DMA((2 * n,))],
                    input_output_aliases={n + 1: 0, n + 2: 1} if outs else {},
                )
            )
        col_adj1, col_adj0 = outs

        parts = [key for key in (("row", 1), ("col", 1)) if key in sides]
        swaps = [("col", k) for k in range(2, col_bits)] + [("col", 0)]
        swaps += [("row", k) for k in range(2, row_bits)]
        pieces = 2 << len(parts)
        data = (b + 1) * (b // LANES)
        total_rows = -(-data // (8 * pieces)) * 8 * pieces
        n1 = sum(p for p, _, _ in shares)
        keep, send = kernel(
            functools.partial(diag_body, blk, n1),
            s,
            [rows1, rows0, p1, p0, inv1, inv0, cross] + t_other + t_own,
            [f32(total_rows // 2, LANES)] * 2,
            15 * rows * b * b + 15 * b**3,
            scratch_shapes=[pltpu.VMEM((b, b), F32)] * 3
            + [pltpu.VMEM((total_rows, LANES), F32)],
        )
        got = swap("row", send, 0)
        for key in parts:
            keep, send = add_split(keep, got, key, keep.shape[0] // 2)
            got = swap(key[0], send, key[1])
        m = add(keep, got)
        for key in swaps:
            m = add(m, swap(key[0], m, key[1]))
        for key in parts[::-1]:
            m = ordered(key, m, swap(key[0], m, key[1]))
        other = swap("row", m, 0)
        d1, d0 = kernel(
            unpack_body,
            s,
            [m, other],
            [f32(b, b)] * 2,
            scratch_shapes=[pltpu.VMEM((total_rows, LANES), F32)],
        )

        trail = {1: [], 0: []}
        for k, share in enumerate(shares):
            keep, got = t_own[k], t_recv[k]
            for bit in range(1, col_bits):
                keep, send = add_split(keep, got, ("col", bit), blk)
                got = swap("col", send, bit)
            trail[share[0]] += [keep, got]
        row1, q = kernel(
            row1_body, s, [p1, p0, inv1, cross] + trail[1], [f32(blk, b)] * 2, 12 * blk * b * b
        )
        (row0,) = kernel(row0_body, s, [q, inv0] + trail[0], [f32(blk, b)], 6 * blk * b * b)
        return row1, row0, col_adj1, col_adj0, d1, d0

    return body


def solution(mesh):
    return jax.shard_map(
        make_local(mesh.shape["row"], mesh.shape["col"]),
        mesh=mesh,
        in_specs=(
            P("row", "col"),
            P("row", None),
            P("row", None),
            P("col", None),
            P("col", None),
            P(),
            P(),
            P(),
            P(("row", "col"), None),
            P(("row", "col"), None),
        ),
        out_specs=(
            P(("row", "col"), None),
            P(("row", "col"), None),
            P("col", None),
            P("col", None),
            P(),
            P(),
        ),
        check_vma=False,
    )
```

time: 269 us -> 156 us (0.58)
  waiting for transfers between devices: 205 us -> 92.1 us
  starting transfers between devices: 0.31 us -> 31.3 us
  matrix products: 26.3 us -> 0 us
  Pallas kernels: 0 us -> 25.6 us
  between operations: 15.6 us -> 1.13 us
  local copies, waits for them, and re-layouts: 18.7 us -> 4.47 us
    psum x2 -> x0, waiting for transfers between devices: 122 us -> none  [the longest x1 122 us: local(): summed1, summed0 = lax.psum((local1, local0), ('row', 'col'))]
    ppermute x0 -> x28, waiting for transfers between devices: none -> 92.1 us  [swap(): return lax.ppermute(a, axis, [(i, i ^ 1 << bit) for i in range(size)])]
    reduce_scatter x1 -> x0, waiting for transfers between devices: 83 us -> none  [local(): lax.psum_scatter(trailing_term(adj_trailing, both_cols), 'col', scatter_d...]
    ppermute x0 -> x28, starting transfers between devices: none -> 31.3 us  [swap(): return lax.ppermute(a, axis, [(i, i ^ 1 << bit) for i in range(size)])]
    dot_general x9 -> x0, matrix products: 26.3 us -> none  [the longest x1 5.88 us: trailing_term(): return jnp.dot(adj_trailing, columns, preferred_element_type=jnp.float32)]
    pallas_call x0 -> x10, Pallas kernels: none -> 25.6 us  [kernel(): pl.pallas_call(body, in_specs=[SMEM] + specs, out_specs=out_specs, out_sh...]
    unnamed x26 -> x22, local copies, waits for them, and re-layouts: 13.9 us -> 4.08 us
    slice x1 -> x0, local copies, waits for them, and re-layouts: 4.82 us -> none  [local(): col_adj0 = column_sum[:, width:]]
  transfers between devices with their start and end apart: 3 -> 28, of which waited for: 2 -> 12; matrix products, arithmetic and copies ran while one was open for 12% -> 1% of each run, Pallas kernels for 0% -> 8%
where the time goes in v1:
time: 156 us
  waiting for transfers between devices  92.1 us (59%)
  starting transfers between devices  31.3 us (20%)
  Pallas kernels  25.6 us (16%)
  local copies, waits for them, and re-layouts  4.47 us (3%)
    ppermute x28, waiting for transfers between devices, swap(): return lax.ppermute(a, axis, [(i, i ^ 1 << bit) for i in range(size)])  92.1 us
    ppermute x28, starting transfers between devices, swap(): return lax.ppermute(a, axis, [(i, i ^ 1 << bit) for i in range(size)])  31.3 us
    pallas_call x10, Pallas kernels, kernel(): pl.pallas_call(body, in_specs=[SMEM] + specs, out_specs=out_specs, out_sh...  25.6 us
    unnamed x22, local copies, waits for them, and re-layouts  4.08 us
  transfers between devices with their start and end apart: 28, of which 12 were waited for; matrix products, arithmetic and copies ran while one was open for 1% of the time, Pallas kernels for 8%

profile of v1, /device:TPU:0, one launch (start us, length us, event | category | flops | bytes accessed | tf_op | source)
XLA Modules:
  0.0 155.9 jit_solution(11640115931762110987)
XLA Ops:
  0.8 1.6 %copy-done = bf16[1024,1024]{1,0:T(8,128)(2,1)S(1)} copy-done((bf16[1024,1024]{1,0:T(8,128)(2,1)S(1)}, bf16[1024,1024]{1,0:T(8,128)(2,1)}, u32[]{:S(2)}) %copy-start) | copy-done | bytes 2097176
  2.4 1.2 copy-done.9
  3.6 1.2 copy-done.10
  4.9 3.6 %shard_map.145 = (f32[512,256]{1,0:T(8,128)S(1)}, f32[512,256]{1,0:T(8,128)S(1)}, f32[512,256]{1,0:T(8,128)S(1)}, f32[512,256]{1,0:T(8,128)S(1)}, f32[512,256]{1...) custom-call(s32[5]{0:T(128)S(1)} %stack.23.s, ...), custom_call_target="tpu_custom_call" | custom-call | flops 2147483648 | bytes 4194304 | tf_op jit(solution)/shard_map/pallas_call | solution.py:57
  8.6 7.9 %shard_map.153 = (f32[1056,128]{1,0:T(8,128)S(1)}, f32[1056,128]{1,0:T(8,128)S(1)}) custom-call(s32[5]{0:T(128)S(1)} %stack.23.s, bf16[1024,512]{1,0:T(8,128)(2,1)S(1)} %copy-done.2, bf16[1024,512]{1,0:T(8,128)(2,1)S(1)} %copy-done.3, bf16[128,512]{1,0:T(8,128)(2,1)S(1)} %copy-done.7, bf16[128,512]{1,0:T(8,128)(2,1)S(1)} %copy-done.8, ...), custom_call_target="tpu_custom_call" | custom-call | flops 6039797760 | bytes 9699328 | tf_op jit(solution)/shard_map/pallas_call | solution.py:57
  16.5 0.6 collective-permute-start.20
  17.1 2.6 %collective-permute-start = (f32[512,256]{1,0:T(8,128)S(1)}, f32[512,256]{1,0:T(8,128)S(1)}, u32[]{:S(2)}, u32[]{:S(2)}) collective-permute-start(f32[512,256]{1,0:T(8,128)S(1)} %get-tuple-element.37.refs_0_), channel_id=1, source_target_pairs={{0,1},{1,0},{2,3},{3,2},{4,5},{5,4},{6,7},{7,6},{8,9},{9,8},{10,11... | collective-permute-start | bytes 1572872 | tf_op jit(solution)/shard_map/ppermute | solution.py:259
  19.7 1.0 shard_map.150
  20.7 0.2 collective-permute-start.15
  20.9 0.3 collective-permute-start.3
  21.2 1.7 %collective-permute-start.6 = (f32[512,256]{1,0:T(8,128)S(1)}, f32[512,256]{1,0:T(8,128)S(1)}, u32[]{:S(2)}, u32[]{:S(2)}) collective-permute-start(f32[512,256]{1,0:T(8,128)S(1)} %get-tuple-element.47.refs_2_), channel_id=1, source_target_pairs={{0,1},{1,0},{2,3},{3,2},{4,5},{5,4},{6,7},{7,6},{8,9},{9,8},{10,11... | collective-permute-start | bytes 1572872 | tf_op jit(solution)/shard_map/ppermute | solution.py:259
  23.0 2.4 %shard_map.148 = (f32[384,1024]{1,0:T(8,128)S(1)}, f32[384,1024]{1,0:T(8,128)S(1)}) custom-call(s32[5]{0:T(128)S(1)} %stack.23.s, bf16[1024,1024]{1,0:T(8,128)(2,1)S(1)} %copy-done.1, bf16[1024,512]{1,0:T(8,128)(2,1)S(1)} %copy-done.2, bf16[1024,512]{1,0:T(8,128)(2,1)S(1)} %copy-done.3), custom_call_target="tpu_custom_call" | custom-call | flops 1610612736 | bytes 4194304 | tf_op jit(solution)/shard_map/pallas_call | solution.py:57
  25.4 1.6 %collective-permute-start.21 = (f32[528,128]{1,0:T(8,128)S(1)}, f32[528,128]{1,0:T(8,128)S(1)}, u32[]{:S(2)}, u32[]{:S(2)}) collective-permute-start(f32[528,128]{1,0:T(8,128)S(1)} %dynamic-slice_bitcast_fusion), channel_id=1, source_target_pairs={{0,16},{8,24},{16,0},{24,8},{1,17},{9,25},{17,1},{25,9},{2,18},{10... | collective-permute-start | bytes 811016 | tf_op jit(solution)/shard_map/ppermute | solution.py:259
  27.0 1.0 shard_map.149
  28.0 4.4 %collective-permute-done = f32[512,256]{1,0:T(8,128)S(1)} collective-permute-done((f32[512,256]{1,0:T(8,128)S(1)}, f32[512,256]{1,0:T(8,128)S(1)}, u32[]{:S(2)}, u32[]{:S(2)}) %collective-permute-start) | collective-permute-done | bytes 524320 | tf_op jit(solution)/shard_map/ppermute | solution.py:259
  32.5 2.0 %collective-permute-start.9 = (f32[512,256]{1,0:T(8,128)S(1)}, f32[512,256]{1,0:T(8,128)S(1)}, u32[]{:S(2)}, u32[]{:S(2)}) collective-permute-start(f32[512,256]{1,0:T(8,128)S(1)} %get-tuple-element.49.refs_3_), channel_id=1, source_target_pairs={{0,1},{1,0},{2,3},{3,2},{4,5},{5,4},{6,7},{7,6},{8,9},{9,8},{10,11... | collective-permute-start | bytes 1572872 | tf_op jit(solution)/shard_map/ppermute | solution.py:259
  34.7 9.0 %collective-permute-done.3 = f32[512,256]{1,0:T(8,128)S(1)} collective-permute-done((f32[512,256]{1,0:T(8,128)S(1)}, f32[512,256]{1,0:T(8,128)S(1)}, u32[]{:S(2)}, u32[]{:S(2)}) %collective-permute-start.3) | collective-permute-done | bytes 524320 | tf_op jit(solution)/shard_map/ppermute | solution.py:259
  43.7 2.0 %collective-permute-start.16 = (f32[128,1024]{1,0:T(8,128)S(1)}, f32[128,1024]{1,0:T(8,128)S(1)}, u32[]{:S(2)}, u32[]{:S(2)}) collective-permute-start(f32[128,1024]{1,0:T(8,128)S(1)} %add.90), channel_id=1, source_target_pairs={{0,16},{8,24},{16,0},{24,8},{1,17},{9,25},{17,1},{25,9},{2,18},{10... | collective-permute-start | bytes 1572872 | tf_op jit(solution)/shard_map/ppermute | solution.py:259
  45.9 9.1 %collective-permute-done.6 = f32[512,256]{1,0:T(8,128)S(1)} collective-permute-done((f32[512,256]{1,0:T(8,128)S(1)}, f32[512,256]{1,0:T(8,128)S(1)}, u32[]{:S(2)}, u32[]{:S(2)}) %collective-permute-start.6) | collective-permute-done | bytes 524320 | tf_op jit(solution)/shard_map/ppermute | solution.py:259
  54.9 2.1 %collective-permute-start.1 = (f32[256,256]{1,0:T(8,128)S(1)}, f32[256,256]{1,0:T(8,128)S(1)}, u32[]{:S(2)}, u32[]{:S(2)}) collective-permute-start(f32[256,256]{1,0:T(8,128)S(1)} %bitcast.66), channel_id=1, source_target_pairs={{0,2},{1,3},{2,0},{3,1},{4,6},{5,7},{6,4},{7,5},{8,10},{9,11},{10,... | collective-permute-start | bytes 786440 | tf_op jit(solution)/shard_map/ppermute | solution.py:259
  57.3 8.6 %collective-permute-done.9 = f32[512,256]{1,0:T(8,128)S(1)} collective-permute-done((f32[512,256]{1,0:T(8,128)S(1)}, f32[512,256]{1,0:T(8,128)S(1)}, u32[]{:S(2)}, u32[]{:S(2)}) %collective-permute-start.9) | collective-permute-done | bytes 524320 | tf_op jit(solution)/shard_map/ppermute | solution.py:259
  65.9 1.8 %collective-permute-start.4 = (f32[256,256]{1,0:T(8,128)S(1)}, f32[256,256]{1,0:T(8,128)S(1)}, u32[]{:S(2)}, u32[]{:S(2)}) collective-permute-start(f32[256,256]{1,0:T(8,128)S(1)} %bitcast.65), channel_id=1, source_target_pairs={{0,2},{1,3},{2,0},{3,1},{4,6},{5,7},{6,4},{7,5},{8,10},{9,11},{10,... | collective-permute-start | bytes 786440 | tf_op jit(solution)/shard_map/ppermute | solution.py:259
  67.8 0.3 collective-permute-start.7
  68.2 2.9 %collective-permute-start.23 = (f32[264,128]{1,0:T(8,128)S(1)}, f32[264,128]{1,0:T(8,128)S(1)}, u32[]{:S(2)}, u32[]{:S(2)}) collective-permute-start(f32[264,128]{1,0:T(8,128)S(1)} %bitcast_add_fusion.5), channel_id=1, source_target_pairs={{0,4},{1,5},{2,6},{3,7},{4,0},{5,1},{6,2},{7,3},{8,12},{9,13},{10,... | collective-permute-start | bytes 405512 | tf_op jit(solution)/shard_map/ppermute | solution.py:259
  71.1 10.4 %collective-permute-done.23 = f32[264,128]{1,0:T(8,128)S(1)} collective-permute-done((f32[264,128]{1,0:T(8,128)S(1)}, f32[264,128]{1,0:T(8,128)S(1)}, u32[]{:S(2)}, u32[]{:S(2)}) %collective-permute-start.23) | collective-permute-done | bytes 135200 | tf_op jit(solution)/shard_map/ppermute | solution.py:259
  81.5 3.5 %collective-permute-start.10 = (f32[256,256]{1,0:T(8,128)S(1)}, f32[256,256]{1,0:T(8,128)S(1)}, u32[]{:S(2)}, u32[]{:S(2)}) collective-permute-start(f32[256,256]{1,0:T(8,128)S(1)} %bitcast.63), channel_id=1, source_target_pairs={{0,2},{1,3},{2,0},{3,1},{4,6},{5,7},{6,4},{7,5},{8,10},{9,11},{10,... | collective-permute-start | bytes 786440 | tf_op jit(solution)/shard_map/ppermute | solution.py:259
  85.1 1.6 %collective-permute-start.24 = (f32[264,128]{1,0:T(8,128)S(1)}, f32[264,128]{1,0:T(8,128)S(1)}, u32[]{:S(2)}, u32[]{:S(2)}) collective-permute-start(f32[264,128]{1,0:T(8,128)S(1)} %add.97), channel_id=1, source_target_pairs={{0,1},{1,0},{2,3},{3,2},{4,5},{5,4},{6,7},{7,6},{8,9},{9,8},{10,11... | collective-permute-start | bytes 405512 | tf_op jit(solution)/shard_map/ppermute | solution.py:259
  86.7 3.5 %collective-permute-done.24 = f32[264,128]{1,0:T(8,128)S(1)} collective-permute-done((f32[264,128]{1,0:T(8,128)S(1)}, f32[264,128]{1,0:T(8,128)S(1)}, u32[]{:S(2)}, u32[]{:S(2)}) %collective-permute-start.24) | collective-permute-done | bytes 135200 | tf_op jit(solution)/shard_map/ppermute | solution.py:259
  90.2 0.2 slice_add_fusion
  90.4 1.6 collective-permute-start.17
  92.0 3.2 %collective-permute-done.25 = f32[264,128]{1,0:T(8,128)S(1)} collective-permute-done((f32[264,128]{1,0:T(8,128)S(1)}, f32[264,128]{1,0:T(8,128)S(1)}, u32[]{:S(2)}, u32[]{:S(2)}) %collective-permute-start.25) | collective-permute-done | bytes 135200 | tf_op jit(solution)/shard_map/ppermute | solution.py:259
  95.3 1.6 collective-permute-start.26
  96.9 0.6 collective-permute-start.13
  97.7 18.8 %collective-permute-done.17 = f32[256,1024]{1,0:T(8,128)S(1)} collective-permute-done((f32[256,1024]{1,0:T(8,128)S(1)}, f32[256,1024]{1,0:T(8,128)S(1)}, u32[]{:S(2)}, u32[]{:S(2)}) %collective-permute-start.17) | collective-permute-done | bytes 1048608 | tf_op jit(solution)/shard_map/ppermute | solution.py:259
  116.5 1.9 %collective-permute-start.5 = (f32[128,256]{1,0:T(8,128)S(1)}, f32[128,256]{1,0:T(8,128)S(1)}, u32[]{:S(2)}, u32[]{:S(2)}) collective-permute-start(f32[128,256]{1,0:T(8,128)S(1)} %get-tuple-element.80), channel_id=1, source_target_pairs={{0,4},{1,5},{2,6},{3,7},{4,0},{5,1},{6,2},{7,3},{8,12},{9,13},{10,... | collective-permute-start | bytes 393224 | tf_op jit(solution)/shard_map/ppermute | solution.py:259
  118.4 0.2 add.93.refs_1_
  118.6 3.7 %collective-permute-done.26 = f32[528,128]{1,0:T(8,128)S(1)} collective-permute-done((f32[528,128]{1,0:T(8,128)S(1)}, f32[528,128]{1,0:T(8,128)S(1)}, u32[]{:S(2)}, u32[]{:S(2)}) %collective-permute-start.26) | collective-permute-done | bytes 270368 | tf_op jit(solution)/shard_map/ppermute | solution.py:259
  122.4 7.8 %collective-permute-done.13 = f32[128,1024]{1,0:T(8,128)S(1)} collective-permute-done((f32[128,1024]{1,0:T(8,128)S(1)}, f32[128,1024]{1,0:T(8,128)S(1)}, u32[]{:S(2)}, u32[]{:S(2)}) %collective-permute-start.13) | collective-permute-done | bytes 524320 | tf_op jit(solution)/shard_map/ppermute | solution.py:259
  130.2 0.6 collective-permute-start.27
  130.8 0.1 collective-permute-start.14
  130.9 1.7 %collective-permute-start.8 = (f32[128,256]{1,0:T(8,128)S(1)}, f32[128,256]{1,0:T(8,128)S(1)}, u32[]{:S(2)}, u32[]{:S(2)}) collective-permute-start(f32[128,256]{1,0:T(8,128)S(1)} %get-tuple-element.78), channel_id=1, source_target_pairs={{0,4},{1,5},{2,6},{3,7},{4,0},{5,1},{6,2},{7,3},{8,12},{9,13},{10,... | collective-permute-start | bytes 393224 | tf_op jit(solution)/shard_map/ppermute | solution.py:259
  132.7 7.8 %collective-permute-done.8.refs_1_ = f32[128,256]{1,0:T(8,128)S(1)} collective-permute-done((f32[128,256]{1,0:T(8,128)S(1)}, f32[128,256]{1,0:T(8,128)S(1)}, u32[]{:S(2)}, u32[]{:S(2)}) %collective-permute-start.8) | collective-permute-done | bytes 131104 | tf_op jit(solution)/shard_map/ppermute | solution.py:259
  140.5 1.8 %shard_map.146 = (f32[128,512]{1,0:T(8,128)}, f32[128,512]{1,0:T(8,128)S(1)}) custom-call(s32[5]{0:T(128)S(1)} %stack.23.s, bf16[128,512]{1,0:T(8,128)(2,1)S(1)} %copy-done.7, bf16[128,512]{1,0:T(8,128)(2,1)S(1)} %copy-done.8, f32[512,512]{1,0:T(8,128)S(1)} %copy-done.4, f32[512,512]{1,0:T(8,128)S(1)} %copy-done.5, ...), custom_call_target="tpu_custom_call" | custom-call | flops 402653184 | bytes 2883584 | tf_op jit(solution)/shard_map/pallas_call | solution.py:57
  142.4 5.7 %collective-permute-done.11.refs_3_ = f32[128,256]{1,0:T(8,128)S(1)} collective-permute-done((f32[128,256]{1,0:T(8,128)S(1)}, f32[128,256]{1,0:T(8,128)S(1)}, u32[]{:S(2)}, u32[]{:S(2)}) %collective-permute-start.11) | collective-permute-done | bytes 131104 | tf_op jit(solution)/shard_map/ppermute | solution.py:259
  148.1 1.7 %shard_map.147 = f32[128,512]{1,0:T(8,128)} custom-call(s32[5]{0:T(128)S(1)} %stack.23.s, f32[128,512]{1,0:T(8,128)S(1)} %get-tuple-element.45.q_ref, f32[512,512]{1,0:T(8,128)S(1)} %copy-done.6, f32[128,256]{1,0:T(8,128)S(1)} %get-tuple-element.79.refs_0_, f32[128,256]{1,0:T(8,128)S(1)} %collective-permute-done.8.refs_1_, ...), custom_call_target="tpu_custom_call" | custom-call | flops 201326592 | bytes 1835008 | tf_op jit(solution)/shard_map/pallas_call | solution.py:57
  149.8 2.2 %shard_map.154 = (f32[512,512]{1,0:T(8,128)}, f32[512,512]{1,0:T(8,128)}) custom-call(s32[5]{0:T(128)S(1)} %stack.23.s, f32[1056,128]{1,0:T(8,128)S(1)} %pad_maximum_fusion.m_ref, f32[1056,128]{1,0:T(8,128)S(1)} %collective-permute-done.27.t_ref), custom_call_target="tpu_custom_call" | custom-call | bytes 1081344 | tf_op jit(solution)/shard_map/pallas_call | solution.py:57
  152.0 2.3 %shard_map.151 = (f32[1024,512]{1,0:T(8,128)}, f32[1024,512]{1,0:T(8,128)}) custom-call(s32[5]{0:T(128)S(1)} %stack.23.s, f32[128,1024]{1,0:T(8,128)S(1)} %add.91.refs_0_, f32[256,1024]{1,0:T(8,128)S(1)} %add.93.refs_1_, f32[128,1024]{1,0:T(8,128)S(1)} %collective-permute-done.18.refs_2_, f32[256,1024]{1,0:T(8,128)S(1)} %collective-permute-done.19.refs_3_), custom_call_target="tpu_custom_call" | custom-call | bytes 3145728 | tf_op jit(solution)/shard_map/pallas_call | solution.py:57
  154.3 1.5 shard_map.152
  (74 shorter events, 1.7 us)
Async XLA Ops:
  0.8 1.6 %copy-start = (bf16[1024,1024]{1,0:T(8,128)(2,1)S(1)}, bf16[1024,1024]{1,0:T(8,128)(2,1)}, u32[]{:S(2)}) copy-start(bf16[1024,1024]{1,0:T(8,128)(2,1)} %a_ref.5) | copy-start | bytes 6291460
  2.4 1.2 copy-start.9
  3.6 1.2 copy-start.10
  4.8 3.7 %copy-start.2 = (bf16[1024,512]{1,0:T(8,128)(2,1)S(1)}, bf16[1024,512]{1,0:T(8,128)(2,1)}, u32[]{:S(2)}) copy-start(bf16[1024,512]{1,0:T(8,128)(2,1)} %r1_ref.7) | copy-start | bytes 3145732
  4.8 3.7 %copy-start.3 = (bf16[1024,512]{1,0:T(8,128)(2,1)S(1)}, bf16[1024,512]{1,0:T(8,128)(2,1)}, u32[]{:S(2)}) copy-start(bf16[1024,512]{1,0:T(8,128)(2,1)} %r0_ref.7) | copy-start | bytes 3145732
  4.8 3.7 %copy-start.4 = (f32[512,512]{1,0:T(8,128)S(1)}, f32[512,512]{1,0:T(8,128)}, u32[]{:S(2)}) copy-start(f32[512,512]{1,0:T(8,128)} %inv1_ref.3) | copy-start | bytes 3145732
  4.8 3.7 %copy-start.5 = (f32[512,512]{1,0:T(8,128)S(1)}, f32[512,512]{1,0:T(8,128)}, u32[]{:S(2)}) copy-start(f32[512,512]{1,0:T(8,128)} %cross_ref.3) | copy-start | bytes 3145732
  4.8 3.7 %copy-start.6 = (f32[512,512]{1,0:T(8,128)S(1)}, f32[512,512]{1,0:T(8,128)}, u32[]{:S(2)}) copy-start(f32[512,512]{1,0:T(8,128)} %inv0_ref.3) | copy-start | bytes 3145732
  4.8 3.7 %copy-start.7 = (bf16[128,512]{1,0:T(8,128)(2,1)S(1)}, bf16[128,512]{1,0:T(8,128)(2,1)}, u32[]{:S(2)}) copy-start(bf16[128,512]{1,0:T(8,128)(2,1)} %p1_ref.3) | copy-start | bytes 393220
  4.9 3.7 %copy-start.8 = (bf16[128,512]{1,0:T(8,128)(2,1)S(1)}, bf16[128,512]{1,0:T(8,128)(2,1)}, u32[]{:S(2)}) copy-start(bf16[128,512]{1,0:T(8,128)(2,1)} %p0_ref.3) | copy-start | bytes 393220
  8.6 11.1 %copy-start.1 = (bf16[1024,1024]{1,0:T(8,128)(2,1)S(1)}, bf16[1024,1024]{1,0:T(8,128)(2,1)}, u32[]{:S(2)}) copy-start(bf16[1024,1024]{1,0:T(8,128)(2,1)} %a_ref.5) | copy-start | bytes 6291460
  16.5 8.8 %collective-permute-start.20 = (f32[1056,128]{1,0:T(8,128)S(1)}, f32[1056,128]{1,0:T(8,128)S(1)}, u32[]{:S(2)}, u32[]{:S(2)}) collective-permute-start(f32[1056,128]{1,0:T(8,128)S(1)} %get-tuple-element.59), channel_id=1, source_target_pairs={{0,8},{8,0},{16,24},{24,16},{1,9},{9,1},{17,25},{25,17},{2,10},{10... | collective-permute-start | bytes 1622024 | tf_op jit(solution)/shard_map/ppermute | solution.py:259
  17.1 15.4 %collective-permute-start = (f32[512,256]{1,0:T(8,128)S(1)}, f32[512,256]{1,0:T(8,128)S(1)}, u32[]{:S(2)}, u32[]{:S(2)}) collective-permute-start(f32[512,256]{1,0:T(8,128)S(1)} %get-tuple-element.37.refs_0_), channel_id=1, source_target_pairs={{0,1},{1,0},{2,3},{3,2},{4,5},{5,4},{6,7},{7,6},{8,9},{9,8},{10,11... | collective-permute-start | bytes 1572872 | tf_op jit(solution)/shard_map/ppermute | solution.py:259
  20.7 13.8 %collective-permute-start.15 = (f32[128,1024]{1,0:T(8,128)S(1)}, f32[128,1024]{1,0:T(8,128)S(1)}, u32[]{:S(2)}, u32[]{:S(2)}) collective-permute-start(f32[128,1024]{1,0:T(8,128)S(1)} %shard_map.150), channel_id=1, source_target_pairs={{0,8},{8,0},{16,24},{24,16},{1,9},{9,1},{17,25},{25,17},{2,10},{10... | collective-permute-start | bytes 1572872 | tf_op jit(solution)/shard_map/ppermute | solution.py:259
  20.9 22.8 %collective-permute-start.3 = (f32[512,256]{1,0:T(8,128)S(1)}, f32[512,256]{1,0:T(8,128)S(1)}, u32[]{:S(2)}, u32[]{:S(2)}) collective-permute-start(f32[512,256]{1,0:T(8,128)S(1)} %get-tuple-element.43.refs_1_), channel_id=1, source_target_pairs={{0,1},{1,0},{2,3},{3,2},{4,5},{5,4},{6,7},{7,6},{8,9},{9,8},{10,11... | collective-permute-start | bytes 1572872 | tf_op jit(solution)/shard_map/ppermute | solution.py:259
  21.2 33.7 %collective-permute-start.6 = (f32[512,256]{1,0:T(8,128)S(1)}, f32[512,256]{1,0:T(8,128)S(1)}, u32[]{:S(2)}, u32[]{:S(2)}) collective-permute-start(f32[512,256]{1,0:T(8,128)S(1)} %get-tuple-element.47.refs_2_), channel_id=1, source_target_pairs={{0,1},{1,0},{2,3},{3,2},{4,5},{5,4},{6,7},{7,6},{8,9},{9,8},{10,11... | collective-permute-start | bytes 1572872 | tf_op jit(solution)/shard_map/ppermute | solution.py:259
  25.4 31.6 %collective-permute-start.21 = (f32[528,128]{1,0:T(8,128)S(1)}, f32[528,128]{1,0:T(8,128)S(1)}, u32[]{:S(2)}, u32[]{:S(2)}) collective-permute-start(f32[528,128]{1,0:T(8,128)S(1)} %dynamic-slice_bitcast_fusion), channel_id=1, source_target_pairs={{0,16},{8,24},{16,0},{24,8},{1,17},{9,25},{17,1},{25,9},{2,18},{10... | collective-permute-start | bytes 811016 | tf_op jit(solution)/shard_map/ppermute | solution.py:259
  32.5 33.4 %collective-permute-start.9 = (f32[512,256]{1,0:T(8,128)S(1)}, f32[512,256]{1,0:T(8,128)S(1)}, u32[]{:S(2)}, u32[]{:S(2)}) collective-permute-start(f32[512,256]{1,0:T(8,128)S(1)} %get-tuple-element.49.refs_3_), channel_id=1, source_target_pairs={{0,1},{1,0},{2,3},{3,2},{4,5},{5,4},{6,7},{7,6},{8,9},{9,8},{10,11... | collective-permute-start | bytes 1572872 | tf_op jit(solution)/shard_map/ppermute | solution.py:259
  34.6 55.7 %collective-permute-start.12 = (f32[384,1024]{1,0:T(8,128)S(1)}, f32[384,1024]{1,0:T(8,128)S(1)}, u32[]{:S(2)}, u32[]{:S(2)}) collective-permute-start(f32[384,1024]{1,0:T(8,128)S(1)} %get-tuple-element.51), channel_id=1, source_target_pairs={{0,8},{8,0},{16,24},{24,16},{1,9},{9,1},{17,25},{25,17},{2,10},{10... | collective-permute-start | bytes 4718600 | tf_op jit(solution)/shard_map/ppermute | solution.py:259
  43.7 53.8 %collective-permute-start.16 = (f32[128,1024]{1,0:T(8,128)S(1)}, f32[128,1024]{1,0:T(8,128)S(1)}, u32[]{:S(2)}, u32[]{:S(2)}) collective-permute-start(f32[128,1024]{1,0:T(8,128)S(1)} %add.90), channel_id=1, source_target_pairs={{0,16},{8,24},{16,0},{24,8},{1,17},{9,25},{17,1},{25,9},{2,18},{10... | collective-permute-start | bytes 1572872 | tf_op jit(solution)/shard_map/ppermute | solution.py:259
  54.9 13.2 %collective-permute-start.1 = (f32[256,256]{1,0:T(8,128)S(1)}, f32[256,256]{1,0:T(8,128)S(1)}, u32[]{:S(2)}, u32[]{:S(2)}) collective-permute-start(f32[256,256]{1,0:T(8,128)S(1)} %bitcast.66), channel_id=1, source_target_pairs={{0,2},{1,3},{2,0},{3,1},{4,6},{5,7},{6,4},{7,5},{8,10},{9,11},{10,... | collective-permute-start | bytes 786440 | tf_op jit(solution)/shard_map/ppermute | solution.py:259
  57.2 10.7 %collective-permute-start.22 = (f32[264,128]{1,0:T(8,128)S(1)}, f32[264,128]{1,0:T(8,128)S(1)}, u32[]{:S(2)}, u32[]{:S(2)}) collective-permute-start(f32[264,128]{1,0:T(8,128)S(1)} %dynamic-slice_bitcast_fusion.1), channel_id=1, source_target_pairs={{0,2},{1,3},{2,0},{3,1},{4,6},{5,7},{6,4},{7,5},{8,10},{9,11},{10,... | collective-permute-start | bytes 405512 | tf_op jit(solution)/shard_map/ppermute | solution.py:259
  65.9 19.1 %collective-permute-start.4 = (f32[256,256]{1,0:T(8,128)S(1)}, f32[256,256]{1,0:T(8,128)S(1)}, u32[]{:S(2)}, u32[]{:S(2)}) collective-permute-start(f32[256,256]{1,0:T(8,128)S(1)} %bitcast.65), channel_id=1, source_target_pairs={{0,2},{1,3},{2,0},{3,1},{4,6},{5,7},{6,4},{7,5},{8,10},{9,11},{10,... | collective-permute-start | bytes 786440 | tf_op jit(solution)/shard_map/ppermute | solution.py:259
  67.8 24.1 %collective-permute-start.7 = (f32[256,256]{1,0:T(8,128)S(1)}, f32[256,256]{1,0:T(8,128)S(1)}, u32[]{:S(2)}, u32[]{:S(2)}) collective-permute-start(f32[256,256]{1,0:T(8,128)S(1)} %bitcast.64), channel_id=1, source_target_pairs={{0,2},{1,3},{2,0},{3,1},{4,6},{5,7},{6,4},{7,5},{8,10},{9,11},{10,... | collective-permute-start | bytes 786440 | tf_op jit(solution)/shard_map/ppermute | solution.py:259
  68.2 13.4 %collective-permute-start.23 = (f32[264,128]{1,0:T(8,128)S(1)}, f32[264,128]{1,0:T(8,128)S(1)}, u32[]{:S(2)}, u32[]{:S(2)}) collective-permute-start(f32[264,128]{1,0:T(8,128)S(1)} %bitcast_add_fusion.5), channel_id=1, source_target_pairs={{0,4},{1,5},{2,6},{3,7},{4,0},{5,1},{6,2},{7,3},{8,12},{9,13},{10,... | collective-permute-start | bytes 405512 | tf_op jit(solution)/shard_map/ppermute | solution.py:259
  81.5 48.7 %collective-permute-start.10 = (f32[256,256]{1,0:T(8,128)S(1)}, f32[256,256]{1,0:T(8,128)S(1)}, u32[]{:S(2)}, u32[]{:S(2)}) collective-permute-start(f32[256,256]{1,0:T(8,128)S(1)} %bitcast.63), channel_id=1, source_target_pairs={{0,2},{1,3},{2,0},{3,1},{4,6},{5,7},{6,4},{7,5},{8,10},{9,11},{10,... | collective-permute-start | bytes 786440 | tf_op jit(solution)/shard_map/ppermute | solution.py:259
  85.1 5.1 %collective-permute-start.24 = (f32[264,128]{1,0:T(8,128)S(1)}, f32[264,128]{1,0:T(8,128)S(1)}, u32[]{:S(2)}, u32[]{:S(2)}) collective-permute-start(f32[264,128]{1,0:T(8,128)S(1)} %add.97), channel_id=1, source_target_pairs={{0,1},{1,0},{2,3},{3,2},{4,5},{5,4},{6,7},{7,6},{8,9},{9,8},{10,11... | collective-permute-start | bytes 405512 | tf_op jit(solution)/shard_map/ppermute | solution.py:259
  90.1 5.1 %collective-permute-start.25 = (f32[264,128]{1,0:T(8,128)S(1)}, f32[264,128]{1,0:T(8,128)S(1)}, u32[]{:S(2)}, u32[]{:S(2)}) collective-permute-start(f32[264,128]{1,0:T(8,128)S(1)} %add.98), channel_id=1, source_target_pairs={{0,2},{1,3},{2,0},{3,1},{4,6},{5,7},{6,4},{7,5},{8,10},{9,11},{10,... | collective-permute-start | bytes 405512 | tf_op jit(solution)/shard_map/ppermute | solution.py:259
  90.4 26.1 %collective-permute-start.17 = (f32[256,1024]{1,0:T(8,128)S(1)}, f32[256,1024]{1,0:T(8,128)S(1)}, u32[]{:S(2)}, u32[]{:S(2)}) collective-permute-start(f32[256,1024]{1,0:T(8,128)S(1)} %slice_add_fusion), channel_id=1, source_target_pairs={{0,16},{8,24},{16,0},{24,8},{1,17},{9,25},{17,1},{25,9},{2,18},{10... | collective-permute-start | bytes 3145736 | tf_op jit(solution)/shard_map/ppermute | solution.py:259
  95.3 27.0 %collective-permute-start.26 = (f32[528,128]{1,0:T(8,128)S(1)}, f32[528,128]{1,0:T(8,128)S(1)}, u32[]{:S(2)}, u32[]{:S(2)}) collective-permute-start(f32[528,128]{1,0:T(8,128)S(1)} %pad_maximum_fusion.1), channel_id=1, source_target_pairs={{0,16},{8,24},{16,0},{24,8},{1,17},{9,25},{17,1},{25,9},{2,18},{10... | collective-permute-start | bytes 811016 | tf_op jit(solution)/shard_map/ppermute | solution.py:259
  96.9 33.2 %collective-permute-start.13 = (f32[128,1024]{1,0:T(8,128)S(1)}, f32[128,1024]{1,0:T(8,128)S(1)}, u32[]{:S(2)}, u32[]{:S(2)}) collective-permute-start(f32[128,1024]{1,0:T(8,128)S(1)} %slice_add_fusion.1), channel_id=1, source_target_pairs={{0,16},{8,24},{16,0},{24,8},{1,17},{9,25},{17,1},{25,9},{2,18},{10... | collective-permute-start | bytes 1572872 | tf_op jit(solution)/shard_map/ppermute | solution.py:259
  97.5 33.3 %collective-permute-start.2 = (f32[128,256]{1,0:T(8,128)S(1)}, f32[128,256]{1,0:T(8,128)S(1)}, u32[]{:S(2)}, u32[]{:S(2)}) collective-permute-start(f32[128,256]{1,0:T(8,128)S(1)} %get-tuple-element.82), channel_id=1, source_target_pairs={{0,4},{1,5},{2,6},{3,7},{4,0},{5,1},{6,2},{7,3},{8,12},{9,13},{10,... | collective-permute-start | bytes 393224 | tf_op jit(solution)/shard_map/ppermute | solution.py:259
  116.5 14.4 %collective-permute-start.5 = (f32[128,256]{1,0:T(8,128)S(1)}, f32[128,256]{1,0:T(8,128)S(1)}, u32[]{:S(2)}, u32[]{:S(2)}) collective-permute-start(f32[128,256]{1,0:T(8,128)S(1)} %get-tuple-element.80), channel_id=1, source_target_pairs={{0,4},{1,5},{2,6},{3,7},{4,0},{5,1},{6,2},{7,3},{8,12},{9,13},{10,... | collective-permute-start | bytes 393224 | tf_op jit(solution)/shard_map/ppermute | solution.py:259
  122.3 29.7 %collective-permute-start.19 = (f32[256,1024]{1,0:T(8,128)S(1)}, f32[256,1024]{1,0:T(8,128)S(1)}, u32[]{:S(2)}, u32[]{:S(2)}) collective-permute-start(f32[256,1024]{1,0:T(8,128)S(1)} %add.93.refs_1_), channel_id=1, source_target_pairs={{0,8},{8,0},{16,24},{24,16},{1,9},{9,1},{17,25},{25,17},{2,10},{10... | collective-permute-start | bytes 3145736 | tf_op jit(solution)/shard_map/ppermute | solution.py:259
  130.1 21.9 %collective-permute-start.18 = (f32[128,1024]{1,0:T(8,128)S(1)}, f32[128,1024]{1,0:T(8,128)S(1)}, u32[]{:S(2)}, u32[]{:S(2)}) collective-permute-start(f32[128,1024]{1,0:T(8,128)S(1)} %add.91.refs_0_), channel_id=1, source_target_pairs={{0,8},{8,0},{16,24},{24,16},{1,9},{9,1},{17,25},{25,17},{2,10},{10... | collective-permute-start | bytes 1572872 | tf_op jit(solution)/shard_map/ppermute | solution.py:259
  130.2 19.6 %collective-permute-start.27 = (f32[1056,128]{1,0:T(8,128)S(1)}, f32[1056,128]{1,0:T(8,128)S(1)}, u32[]{:S(2)}, u32[]{:S(2)}) collective-permute-start(f32[1056,128]{1,0:T(8,128)S(1)} %pad_maximum_fusion.m_ref), channel_id=1, source_target_pairs={{0,8},{8,0},{16,24},{24,16},{1,9},{9,1},{17,25},{25,17},{2,10},{10... | collective-permute-start | bytes 1622024 | tf_op jit(solution)/shard_map/ppermute | solution.py:259
  130.8 23.5 %collective-permute-start.14 = (f32[128,1024]{1,0:T(8,128)S(1)}, f32[128,1024]{1,0:T(8,128)S(1)}, u32[]{:S(2)}, u32[]{:S(2)}) collective-permute-start(f32[128,1024]{1,0:T(8,128)S(1)} %add.89.refs_0_), channel_id=1, source_target_pairs={{0,8},{8,0},{16,24},{24,16},{1,9},{9,1},{17,25},{25,17},{2,10},{10... | collective-permute-start | bytes 1572872 | tf_op jit(solution)/shard_map/ppermute | solution.py:259
  130.9 9.6 %collective-permute-start.8 = (f32[128,256]{1,0:T(8,128)S(1)}, f32[128,256]{1,0:T(8,128)S(1)}, u32[]{:S(2)}, u32[]{:S(2)}) collective-permute-start(f32[128,256]{1,0:T(8,128)S(1)} %get-tuple-element.78), channel_id=1, source_target_pairs={{0,4},{1,5},{2,6},{3,7},{4,0},{5,1},{6,2},{7,3},{8,12},{9,13},{10,... | collective-permute-start | bytes 393224 | tf_op jit(solution)/shard_map/ppermute | solution.py:259
  140.5 7.6 %collective-permute-start.11 = (f32[128,256]{1,0:T(8,128)S(1)}, f32[128,256]{1,0:T(8,128)S(1)}, u32[]{:S(2)}, u32[]{:S(2)}) collective-permute-start(f32[128,256]{1,0:T(8,128)S(1)} %get-tuple-element.76), channel_id=1, source_target_pairs={{0,4},{1,5},{2,6},{3,7},{4,0},{5,1},{6,2},{7,3},{8,12},{9,13},{10,... | collective-permute-start | bytes 393224 | tf_op jit(solution)/shard_map/ppermute | solution.py:259

commit v2 on v1

--- a/solution.py
+++ b/solution.py
@@ -11,8 +11,8 @@
 BF16 = jnp.bfloat16
 LANES = 128
 
-T_SHARES = ((1, 0, 4), (1, 4, 4), (0, 0, 4), (0, 4, 4))
-C_SHARES = ((0, 2), (2, 4), (6, 2))
+T_SHARES = ((1, 0, 6), (1, 6, 2), (0, 0, 4), (0, 4, 2), (0, 6, 2))
+C_BLOCKS = ((0, 2, 1), (2, 6, 3))
 
 
 def mm(a, b):
@@ -26,13 +26,6 @@
 def split2(x):
     hi = x.astype(BF16)
     return hi, (x - hi.astype(F32)).astype(BF16)
-
-
-def split3(x):
-    hi = x.astype(BF16)
-    rest = x - hi.astype(F32)
-    mid = rest.astype(BF16)
-    return hi, mid, (rest - mid.astype(F32)).astype(BF16)
 
 
 def mm3(a, b):
@@ -78,10 +71,6 @@
     )
 
 
-def trail_block(a, c_ref, start, o_ref):
-    o_ref[...] = mm(a, c_ref[:, start : start + o_ref.shape[1]])
-
-
 def column_block(at, r1_ref, r0_ref, o_ref):
     b = r1_ref.shape[1]
     o_ref[:, :b] = -mm_t(at, r1_ref[...])
@@ -120,29 +109,32 @@
     load_cols("c1", c1_hbm, c1_ref)
     load_cols("c0", c0_hbm, c0_ref)
     load_rows(1)
-    for (own, panel, start), o_ref in zip(plan, o_refs):
+    for half in sorted({(own, 1 - panel) for own, panel, _ in plan}):
+        own, panel = half[0], 1 - half[1]
         for key in (own, "c1" if panel else "c0"):
             for c in loads[key]:
                 c.wait()
             loads[key] = []
-        trail_block(a_ref[own], c1_ref if panel else c0_ref, start, o_ref)
-
-
-def column_body(sides, plan, s, a_ref, r1_ref, r0_ref, *o_refs):
+        t = mm(a_ref[own], (c1_ref if panel else c0_ref)[...])
+        for (*key, start), o_ref in zip(plan, o_refs):
+            if key == [own, panel]:
+                o_ref[...] = t[:, start : start + o_ref.shape[1]]
+
+
+def column_body(sides, start, s, a_ref, r1_ref, r0_ref, *o_refs):
     for own, o_ref in zip(sides, o_refs):
         side = s[CORE] if own else 1 - s[CORE]
-        at = [window_cols(a_ref, start, side, half) for start, half in plan]
-        column_block(jnp.concatenate(at, axis=1), r1_ref, r0_ref, o_ref)
-
-
-def write_body(starts, s, *refs):
-    n = len(starts)
+        column_block(window_cols(a_ref, start, side, o_ref.shape[0]), r1_ref, r0_ref, o_ref)
+
+
+def write_body(places, s, *refs):
+    n = len(places)
     d1_ref, d0_ref, sem = refs[-3:]
     copies = []
-    for k, start in enumerate(starts):
+    for k, (start, stride) in enumerate(places):
         for ref, side in ((refs[k], s[CORE]), (refs[n + k], 1 - s[CORE])):
             half, b = ref.shape[0], ref.shape[1] // 2
-            at = pl.ds(pl.multiple_of(start + side * half, 8), half)
+            at = pl.ds(pl.multiple_of(start + side * stride, 8), half)
             for lanes, out in ((slice(0, b), d1_ref), (slice(b, 2 * b), d0_ref)):
                 copies.append(
                     pltpu.make_async_copy(ref.at[:, lanes], out.at[at], sem.at[len(copies)])
@@ -180,12 +172,12 @@
                 bar = bar + jnp.where(place, jnp.concatenate([p] * (n // blk), axis=0), 0.0)
             for side in (0, 1):
                 at = slice(side * h, (side + 1) * h)
-                parts = jnp.concatenate(split3(bar[:, at]), axis=1)
+                parts = jnp.concatenate(split2(bar[:, at]), axis=1)
                 top = b if side else h
                 todo = [(g1, r1[:, :top]), (g10, r0)] if panel else [(g0, r0[:, :top])]
                 for g, r in todo:
                     x = mm_t(r, parts)
-                    x = x[:, :h] + (x[:, h : 2 * h] + x[:, 2 * h :])
+                    x = x[:, :h] + x[:, h:]
                     k = r.shape[1]
                     if own:
                         x = x + g[:k, at]
@@ -298,14 +290,14 @@
 
         half_rows = rows // 2
         shares = [(p, st * b // 8, w * b // 8) for p, st, w in T_SHARES]
-        windows = [(st * window // 8, w * window // 16) for st, w in C_SHARES]
+        blocks = [(st * window // 8, w * window // 16, cuts) for st, w, cuts in C_BLOCKS]
 
         nt = len(shares)
         plan = [(own, p, st) for own in (0, 1) for p, st, _ in shares]
         out = kernel(
             functools.partial(trail_body, blk, plan),
             s,
-            [adj, cols1, cols0],
+            [pltpu.with_memory_space_constraint(x, pltpu.HBM) for x in (adj, cols1, cols0)],
             [f32(half_rows, w) for _, _, w in shares + shares],
             4 * rows * window * b,
             specs=[pl.BlockSpec(memory_space=pltpu.HBM)] * 3,
@@ -319,26 +311,27 @@
         t_other, t_own = list(out[:nt]), list(out[nt:])
         t_recv = [swap("col", t, 0) for t in t_other]
 
-        def columns(sides, some):
-            width = sum(w for _, w in some)
+        def columns(sides, block):
             return kernel(
-                functools.partial(column_body, sides, some),
+                functools.partial(column_body, sides, block[0]),
                 s,
                 [adj, rows1, rows0],
-                [f32(width, 2 * b)] * len(sides),
-                len(sides) * 4 * rows * width * b,
+                [f32(block[1], 2 * b)] * len(sides),
+                len(sides) * 4 * rows * block[1] * b,
             )
 
-        (c_other,) = columns((0,), windows[:1])
-        c_recv = swap("row", c_other, 0)
-        (c_own,) = columns((1,), windows[:1])
-        sums = [add(c_own, c_recv)]
-        c_other, c_own = columns((0, 1), windows[1:])
-        c_recv = swap("row", c_other, 0)
-        at = 0
-        for _, w in windows[1:]:
-            sums.append(c_own[at : at + w] + c_recv[at : at + w])
-            at += w
+        sums, places = [], []
+        for k, block in enumerate(blocks):
+            if k == 0:
+                (c_other,), (c_own,) = columns((0,), block), columns((1,), block)
+            else:
+                c_other, c_own = columns((0, 1), block)
+            c_recv = swap("row", c_other, 0)
+            start, half, cuts = block
+            for at in range(0, half, half // cuts):
+                cut = slice(at, at + half // cuts)
+                sums.append(add(c_own[cut], c_recv[cut]))
+                places.append((start + at, half))
 
         held, theirs = [], []
         for total in sums:
@@ -347,12 +340,12 @@
             held.append(total)
             theirs.append(swap("row", total, 0))
         outs = []
-        for ks in (range(len(sums) - 1), range(len(sums) - 1, len(sums))):
+        for ks in (range(len(sums) // 2), range(len(sums) // 2, len(sums))):
             args = [held[k] for k in ks] + [theirs[k] for k in ks]
             n = len(args)
             outs = list(
                 kernel(
-                    functools.partial(write_body, [windows[k][0] for k in ks]),
+                    functools.partial(write_body, [places[k] for k in ks]),
                     s,
                     args + outs,
                     [f32(window, b)] * 2,
@@ -364,9 +357,8 @@
             )
         col_adj1, col_adj0 = outs
 
-        parts = [key for key in (("row", 1), ("col", 1)) if key in sides]
-        swaps = [("col", k) for k in range(2, col_bits)] + [("col", 0)]
-        swaps += [("row", k) for k in range(2, row_bits)]
+        parts = [("col", k) for k in (1, 0) if k < col_bits]
+        swaps = [("col", k) for k in range(2, col_bits)] + [("row", k) for k in range(1, row_bits)]
         pieces = 2 << len(parts)
         data = (b + 1) * (b // LANES)
         total_rows = -(-data // (8 * pieces)) * 8 * pieces
@@ -387,8 +379,10 @@
         m = add(keep, got)
         for key in swaps:
             m = add(m, swap(key[0], m, key[1]))
-        for key in parts[::-1]:
+        for key in parts:
             m = ordered(key, m, swap(key[0], m, key[1]))
+        if len(parts) == 2:
+            m = m.reshape(2, 2, -1, LANES).swapaxes(0, 1).reshape(-1, LANES)
         other = swap("row", m, 0)
         d1, d0 = kernel(
             unpack_body,

time: 156 us -> 129 us (0.83)
  waiting for transfers between devices: 92.1 us -> 67.2 us
  local copies, waits for them, and re-layouts: 4.47 us -> 0.47 us
  starting transfers between devices: 31.3 us -> 32.9 us
    ppermute x28 -> x33, waiting for transfers between devices: 92.1 us -> 67.2 us  [swap(): return lax.ppermute(a, axis, [(i, i ^ 1 << bit) for i in range(size)])]
    unnamed x22 -> x16, local copies, waits for them, and re-layouts: 4.08 us -> 0.04 us
    ppermute x28 -> x33, starting transfers between devices: 31.3 us -> 32.9 us  [swap(): return lax.ppermute(a, axis, [(i, i ^ 1 << bit) for i in range(size)])]
  transfers between devices with their start and end apart: 28 -> 33, of which waited for: 12 -> 14; matrix products, arithmetic and copies ran while one was open for 1% -> 1% of each run, Pallas kernels for 8% -> 14%
where the time goes in v2:
time: 129 us
  waiting for transfers between devices  67.2 us (52%)
  starting transfers between devices  32.9 us (26%)
  Pallas kernels  25.7 us (20%)
    ppermute x33, waiting for transfers between devices, swap(): return lax.ppermute(a, axis, [(i, i ^ 1 << bit) for i in range(size)])  67.2 us
    ppermute x33, starting transfers between devices, swap(): return lax.ppermute(a, axis, [(i, i ^ 1 << bit) for i in range(size)])  32.9 us
    pallas_call x10, Pallas kernels, kernel(): pl.pallas_call(body, in_specs=[SMEM] + specs, out_specs=out_specs, out_sh...  25.7 us
  transfers between devices with their start and end apart: 33, of which 14 were waited for; matrix products, arithmetic and copies ran while one was open for 1% of the time, Pallas kernels for 14%

profile of v2, /device:TPU:0, one launch (start us, length us, event | category | flops | bytes accessed | tf_op | source)
XLA Modules:
  0.0 128.5 jit_solution(5086664186201331879)
XLA Ops:
  0.8 5.1 %shard_map.145 = (f32[512,384]{1,0:T(8,128)S(1)}, f32[512,128]{1,0:T(8,128)S(1)}, f32[512,256]{1,0:T(8,128)S(1)}, f32[512,128]{1,0:T(8,128)S(1)}, f32[512,128]{1...) custom-call(s32[5]{0:T(128)S(1)} %stack.23.s, ...), custom_call_target="tpu_custom_call" | custom-call | flops 2147483648 | bytes 4194304 | tf_op jit(solution)/shard_map/pallas_call | solution.py:50
  6.0 3.1 %collective-permute-start.3 = (f32[512,128]{1,0:T(8,128)S(1)}, f32[512,128]{1,0:T(8,128)S(1)}, u32[]{:S(2)}, u32[]{:S(2)}) collective-permute-start(f32[512,128]{1,0:T(8,128)S(1)} %get-tuple-element.45.refs_1_), channel_id=1, source_target_pairs={{0,1},{1,0},{2,3},{3,2},{4,5},{5,4},{6,7},{7,6},{8,9},{9,8},{10,11... | collective-permute-start | bytes 786440 | tf_op jit(solution)/shard_map/ppermute | solution.py:251
  9.1 1.9 %collective-permute-start.12 = (f32[512,128]{1,0:T(8,128)S(1)}, f32[512,128]{1,0:T(8,128)S(1)}, u32[]{:S(2)}, u32[]{:S(2)}) collective-permute-start(f32[512,128]{1,0:T(8,128)S(1)} %get-tuple-element.53.refs_4_), channel_id=1, source_target_pairs={{0,1},{1,0},{2,3},{3,2},{4,5},{5,4},{6,7},{7,6},{8,9},{9,8},{10,11... | collective-permute-start | bytes 786440 | tf_op jit(solution)/shard_map/ppermute | solution.py:251
  11.1 1.9 %collective-permute-start = (f32[512,384]{1,0:T(8,128)S(1)}, f32[512,384]{1,0:T(8,128)S(1)}, u32[]{:S(2)}, u32[]{:S(2)}) collective-permute-start(f32[512,384]{1,0:T(8,128)S(1)} %get-tuple-element.39.refs_0_), channel_id=1, source_target_pairs={{0,1},{1,0},{2,3},{3,2},{4,5},{5,4},{6,7},{7,6},{8,9},{9,8},{10,11... | collective-permute-start | bytes 2359304 | tf_op jit(solution)/shard_map/ppermute | solution.py:251
  13.1 6.5 %shard_map.153 = (f32[1056,128]{1,0:T(8,128)S(1)}, f32[1056,128]{1,0:T(8,128)S(1)}) custom-call(s32[5]{0:T(128)S(1)} %stack.23.s, bf16[1024,512]{1,0:T(8,128)(2,1)S(1)} %copy-done.1, bf16[1024,512]{1,0:T(8,128)(2,1)S(1)} %copy-done.2, bf16[128,512]{1,0:T(8,128)(2,1)S(1)} %copy-done.6, bf16[128,512]{1,0:T(8,128)(2,1)S(1)} %copy-done.7, ...), custom_call_target="tpu_custom_call" | custom-call | flops 6039797760 | bytes 9699328 | tf_op jit(solution)/shard_map/pallas_call | solution.py:50
  19.7 1.0 shard_map.150
  20.7 2.4 %shard_map.148 = (f32[384,1024]{1,0:T(8,128)S(1)}, f32[384,1024]{1,0:T(8,128)S(1)}) custom-call(s32[5]{0:T(128)S(1)} %stack.23.s, bf16[1024,1024]{1,0:T(8,128)(2,1)S(1)} %copy-done, bf16[1024,512]{1,0:T(8,128)(2,1)S(1)} %copy-done.1, bf16[1024,512]{1,0:T(8,128)(2,1)S(1)} %copy-done.2), custom_call_target="tpu_custom_call" | custom-call | flops 1610612736 | bytes 4194304 | tf_op jit(solution)/shard_map/pallas_call | solution.py:50
  23.1 1.0 shard_map.149
  24.3 1.7 %collective-permute-start.4 = (f32[256,128]{1,0:T(8,128)S(1)}, f32[256,128]{1,0:T(8,128)S(1)}, u32[]{:S(2)}, u32[]{:S(2)}) collective-permute-start(f32[256,128]{1,0:T(8,128)S(1)} %bitcast.85), channel_id=1, source_target_pairs={{0,2},{1,3},{2,0},{3,1},{4,6},{5,7},{6,4},{7,5},{8,10},{9,11},{10,... | collective-permute-start | bytes 393224 | tf_op jit(solution)/shard_map/ppermute | solution.py:251
  26.0 1.4 %collective-permute-done.12 = f32[512,128]{1,0:T(8,128)S(1)} collective-permute-done((f32[512,128]{1,0:T(8,128)S(1)}, f32[512,128]{1,0:T(8,128)S(1)}, u32[]{:S(2)}, u32[]{:S(2)}) %collective-permute-start.12) | collective-permute-done | bytes 262176 | tf_op jit(solution)/shard_map/ppermute | solution.py:251
  27.5 2.8 %collective-permute-done.4 = f32[256,128]{1,0:T(8,128)S(1)} collective-permute-done((f32[256,128]{1,0:T(8,128)S(1)}, f32[256,128]{1,0:T(8,128)S(1)}, u32[]{:S(2)}, u32[]{:S(2)}) %collective-permute-start.4) | collective-permute-done | bytes 131104 | tf_op jit(solution)/shard_map/ppermute | solution.py:251
  30.3 1.6 %collective-permute-start.10 = (f32[256,128]{1,0:T(8,128)S(1)}, f32[256,128]{1,0:T(8,128)S(1)}, u32[]{:S(2)}, u32[]{:S(2)}) collective-permute-start(f32[256,128]{1,0:T(8,128)S(1)} %bitcast.83), channel_id=1, source_target_pairs={{0,2},{1,3},{2,0},{3,1},{4,6},{5,7},{6,4},{7,5},{8,10},{9,11},{10,... | collective-permute-start | bytes 393224 | tf_op jit(solution)/shard_map/ppermute | solution.py:251
  31.9 0.5 collective-permute-start.13
  32.5 4.2 %collective-permute-done.10 = f32[256,128]{1,0:T(8,128)S(1)} collective-permute-done((f32[256,128]{1,0:T(8,128)S(1)}, f32[256,128]{1,0:T(8,128)S(1)}, u32[]{:S(2)}, u32[]{:S(2)}) %collective-permute-start.10) | collective-permute-done | bytes 131104 | tf_op jit(solution)/shard_map/ppermute | solution.py:251
  36.6 1.6 %collective-permute-start.26 = (f32[528,128]{1,0:T(8,128)S(1)}, f32[528,128]{1,0:T(8,128)S(1)}, u32[]{:S(2)}, u32[]{:S(2)}) collective-permute-start(f32[528,128]{1,0:T(8,128)S(1)} %dynamic-slice_bitcast_fusion), channel_id=1, source_target_pairs={{0,2},{1,3},{2,0},{3,1},{4,6},{5,7},{6,4},{7,5},{8,10},{9,11},{10,... | collective-permute-start | bytes 811016 | tf_op jit(solution)/shard_map/ppermute | solution.py:251
  38.2 1.2 collective-permute-done.13
  39.5 4.4 %collective-permute-done.26 = f32[528,128]{1,0:T(8,128)S(1)} collective-permute-done((f32[528,128]{1,0:T(8,128)S(1)}, f32[528,128]{1,0:T(8,128)S(1)}, u32[]{:S(2)}, u32[]{:S(2)}) %collective-permute-start.26) | collective-permute-done | bytes 270368 | tf_op jit(solution)/shard_map/ppermute | solution.py:251
  44.0 0.7 collective-permute-start.27
  44.8 1.5 %collective-permute-start.7 = (f32[256,256]{1,0:T(8,128)S(1)}, f32[256,256]{1,0:T(8,128)S(1)}, u32[]{:S(2)}, u32[]{:S(2)}) collective-permute-start(f32[256,256]{1,0:T(8,128)S(1)} %bitcast.82), channel_id=1, source_target_pairs={{0,2},{1,3},{2,0},{3,1},{4,6},{5,7},{6,4},{7,5},{8,10},{9,11},{10,... | collective-permute-start | bytes 786440 | tf_op jit(solution)/shard_map/ppermute | solution.py:251
  46.3 11.2 %collective-permute-done.27 = f32[264,128]{1,0:T(8,128)S(1)} collective-permute-done((f32[264,128]{1,0:T(8,128)S(1)}, f32[264,128]{1,0:T(8,128)S(1)}, u32[]{:S(2)}, u32[]{:S(2)}) %collective-permute-start.27) | collective-permute-done | bytes 135200 | tf_op jit(solution)/shard_map/ppermute | solution.py:251
  57.6 2.9 %collective-permute-start.28 = (f32[264,128]{1,0:T(8,128)S(1)}, f32[264,128]{1,0:T(8,128)S(1)}, u32[]{:S(2)}, u32[]{:S(2)}) collective-permute-start(f32[264,128]{1,0:T(8,128)S(1)} %bitcast_add_fusion.3), channel_id=1, source_target_pairs={{0,4},{1,5},{2,6},{3,7},{4,0},{5,1},{6,2},{7,3},{8,12},{9,13},{10,... | collective-permute-start | bytes 405512 | tf_op jit(solution)/shard_map/ppermute | solution.py:251
  60.6 1.6 %collective-permute-start.21 = (f32[128,1024]{1,0:T(8,128)S(1)}, f32[128,1024]{1,0:T(8,128)S(1)}, u32[]{:S(2)}, u32[]{:S(2)}) collective-permute-start(f32[128,1024]{1,0:T(8,128)S(1)} %add.103), channel_id=1, source_target_pairs={{0,16},{8,24},{16,0},{24,8},{1,17},{9,25},{17,1},{25,9},{2,18},{10... | collective-permute-start | bytes 1572872 | tf_op jit(solution)/shard_map/ppermute | solution.py:251
  62.1 4.1 %collective-permute-done.28 = f32[264,128]{1,0:T(8,128)S(1)} collective-permute-done((f32[264,128]{1,0:T(8,128)S(1)}, f32[264,128]{1,0:T(8,128)S(1)}, u32[]{:S(2)}, u32[]{:S(2)}) %collective-permute-start.28) | collective-permute-done | bytes 135200 | tf_op jit(solution)/shard_map/ppermute | solution.py:251
  66.2 1.5 %collective-permute-start.29 = (f32[264,128]{1,0:T(8,128)S(1)}, f32[264,128]{1,0:T(8,128)S(1)}, u32[]{:S(2)}, u32[]{:S(2)}) collective-permute-start(f32[264,128]{1,0:T(8,128)S(1)} %add.110), channel_id=1, source_target_pairs={{0,16},{8,24},{16,0},{24,8},{1,17},{9,25},{17,1},{25,9},{2,18},{10... | collective-permute-start | bytes 405512 | tf_op jit(solution)/shard_map/ppermute | solution.py:251
  67.7 8.3 %collective-permute-done.29 = f32[264,128]{1,0:T(8,128)S(1)} collective-permute-done((f32[264,128]{1,0:T(8,128)S(1)}, f32[264,128]{1,0:T(8,128)S(1)}, u32[]{:S(2)}, u32[]{:S(2)}) %collective-permute-start.29) | collective-permute-done | bytes 135200 | tf_op jit(solution)/shard_map/ppermute | solution.py:251
  76.1 1.6 %collective-permute-start.30 = (f32[264,128]{1,0:T(8,128)S(1)}, f32[264,128]{1,0:T(8,128)S(1)}, u32[]{:S(2)}, u32[]{:S(2)}) collective-permute-start(f32[264,128]{1,0:T(8,128)S(1)} %add.111), channel_id=1, source_target_pairs={{0,2},{1,3},{2,0},{3,1},{4,6},{5,7},{6,4},{7,5},{8,10},{9,11},{10,... | collective-permute-start | bytes 405512 | tf_op jit(solution)/shard_map/ppermute | solution.py:251
  77.9 0.5 collective-permute-start.1
  78.4 4.2 %collective-permute-done.30 = f32[264,128]{1,0:T(8,128)S(1)} collective-permute-done((f32[264,128]{1,0:T(8,128)S(1)}, f32[264,128]{1,0:T(8,128)S(1)}, u32[]{:S(2)}, u32[]{:S(2)}) %collective-permute-start.30) | collective-permute-done | bytes 135200 | tf_op jit(solution)/shard_map/ppermute | solution.py:251
  82.7 1.6 %collective-permute-start.31 = (f32[528,128]{1,0:T(8,128)S(1)}, f32[528,128]{1,0:T(8,128)S(1)}, u32[]{:S(2)}, u32[]{:S(2)}) collective-permute-start(f32[528,128]{1,0:T(8,128)S(1)} %pad_maximum_fusion.1), channel_id=1, source_target_pairs={{0,1},{1,0},{2,3},{3,2},{4,5},{5,4},{6,7},{7,6},{8,9},{9,8},{10,11... | collective-permute-start | bytes 811016 | tf_op jit(solution)/shard_map/ppermute | solution.py:251
  84.2 0.3 slice_add_fusion
  84.5 1.6 %collective-permute-start.22 = (f32[128,1024]{1,0:T(8,128)S(1)}, f32[128,1024]{1,0:T(8,128)S(1)}, u32[]{:S(2)}, u32[]{:S(2)}) collective-permute-start(f32[128,1024]{1,0:T(8,128)S(1)} %get-tuple-element.68), channel_id=1, source_target_pairs={{0,16},{8,24},{16,0},{24,8},{1,17},{9,25},{17,1},{25,9},{2,18},{10... | collective-permute-start | bytes 1572872 | tf_op jit(solution)/shard_map/ppermute | solution.py:251
  86.1 0.5 collective-permute-start.17
  86.6 1.4 %collective-permute-done.1 = f32[256,384]{1,0:T(8,128)S(1)} collective-permute-done((f32[256,384]{1,0:T(8,128)S(1)}, f32[256,384]{1,0:T(8,128)S(1)}, u32[]{:S(2)}, u32[]{:S(2)}) %collective-permute-start.1) | collective-permute-done | bytes 393248 | tf_op jit(solution)/shard_map/ppermute | solution.py:251
  88.1 1.5 %collective-permute-start.16 = (f32[128,1024]{1,0:T(8,128)S(1)}, f32[128,1024]{1,0:T(8,128)S(1)}, u32[]{:S(2)}, u32[]{:S(2)}) collective-permute-start(f32[128,1024]{1,0:T(8,128)S(1)} %get-tuple-element.70), channel_id=1, source_target_pairs={{0,16},{8,24},{16,0},{24,8},{1,17},{9,25},{17,1},{25,9},{2,18},{10... | collective-permute-start | bytes 1572872 | tf_op jit(solution)/shard_map/ppermute | solution.py:251
  89.6 0.4 collective-permute-start.5
  90.1 9.0 %collective-permute-done.5.refs_3_ = f32[128,128]{1,0:T(8,128)S(1)} collective-permute-done((f32[128,128]{1,0:T(8,128)S(1)}, f32[128,128]{1,0:T(8,128)S(1)}, u32[]{:S(2)}, u32[]{:S(2)}) %collective-permute-start.5) | collective-permute-done | bytes 65568 | tf_op jit(solution)/shard_map/ppermute | solution.py:251
  99.1 2.9 %collective-permute-start.14 = (f32[128,128]{1,0:T(8,128)S(1)}, f32[128,128]{1,0:T(8,128)S(1)}, u32[]{:S(2)}, u32[]{:S(2)}) collective-permute-start(f32[128,128]{1,0:T(8,128)S(1)} %get-tuple-element.89), channel_id=1, source_target_pairs={{0,4},{1,5},{2,6},{3,7},{4,0},{5,1},{6,2},{7,3},{8,12},{9,13},{10,... | collective-permute-start | bytes 196616 | tf_op jit(solution)/shard_map/ppermute | solution.py:251
  102.1 8.1 %collective-permute-done.17 = f32[128,1024]{1,0:T(8,128)S(1)} collective-permute-done((f32[128,1024]{1,0:T(8,128)S(1)}, f32[128,1024]{1,0:T(8,128)S(1)}, u32[]{:S(2)}, u32[]{:S(2)}) %collective-permute-start.17) | collective-permute-done | bytes 524320 | tf_op jit(solution)/shard_map/ppermute | solution.py:251
  110.2 0.4 collective-permute-start.2
  110.7 5.2 %collective-permute-done.16 = f32[128,1024]{1,0:T(8,128)S(1)} collective-permute-done((f32[128,1024]{1,0:T(8,128)S(1)}, f32[128,1024]{1,0:T(8,128)S(1)}, u32[]{:S(2)}, u32[]{:S(2)}) %collective-permute-start.16) | collective-permute-done | bytes 524320 | tf_op jit(solution)/shard_map/ppermute | solution.py:251
  116.1 0.6 collective-permute-start.23
  116.8 0.4 collective-permute-start.19
  117.2 1.7 %collective-permute-done.2.refs_1_ = f32[128,384]{1,0:T(8,128)S(1)} collective-permute-done((f32[128,384]{1,0:T(8,128)S(1)}, f32[128,384]{1,0:T(8,128)S(1)}, u32[]{:S(2)}, u32[]{:S(2)}) %collective-permute-start.2) | collective-permute-done | bytes 196640 | tf_op jit(solution)/shard_map/ppermute | solution.py:251
  118.9 1.8 %shard_map.146 = (f32[128,512]{1,0:T(8,128)}, f32[128,512]{1,0:T(8,128)S(1)}) custom-call(s32[5]{0:T(128)S(1)} %stack.23.s, bf16[128,512]{1,0:T(8,128)(2,1)S(1)} %copy-done.6, bf16[128,512]{1,0:T(8,128)(2,1)S(1)} %copy-done.7, f32[512,512]{1,0:T(8,128)S(1)} %copy-done.3, f32[512,512]{1,0:T(8,128)S(1)} %copy-done.4, ...), custom_call_target="tpu_custom_call" | custom-call | flops 402653184 | bytes 2883584 | tf_op jit(solution)/shard_map/pallas_call | solution.py:50
  120.7 1.7 %shard_map.147 = f32[128,512]{1,0:T(8,128)} custom-call(s32[5]{0:T(128)S(1)} %stack.23.s, f32[128,512]{1,0:T(8,128)S(1)} %get-tuple-element.47.q_ref, f32[512,512]{1,0:T(8,128)S(1)} %copy-done.5, f32[128,256]{1,0:T(8,128)S(1)} %get-tuple-element.86.refs_0_, f32[128,256]{1,0:T(8,128)S(1)} %collective-permute-done.8.refs_1_, ...), custom_call_target="tpu_custom_call" | custom-call | flops 201326592 | bytes 1835008 | tf_op jit(solution)/shard_map/pallas_call | solution.py:50
  122.5 2.2 %shard_map.154 = (f32[512,512]{1,0:T(8,128)}, f32[512,512]{1,0:T(8,128)}) custom-call(s32[5]{0:T(128)S(1)} %stack.23.s, f32[1056,128]{1,0:T(8,128)S(1)} %bitcast.65, f32[1056,128]{1,0:T(8,128)S(1)} %collective-permute-done.32.t_ref), custom_call_target="tpu_custom_call" | custom-call | bytes 1081344 | tf_op jit(solution)/shard_map/pallas_call | solution.py:50
  124.7 1.9 %shard_map.151 = (f32[1024,512]{1,0:T(8,128)}, f32[1024,512]{1,0:T(8,128)}) custom-call(s32[5]{0:T(128)S(1)} %stack.23.s, f32[128,1024]{1,0:T(8,128)S(1)} %add.104.refs_0_, f32[128,1024]{1,0:T(8,128)S(1)} %add.106.refs_1_, f32[128,1024]{1,0:T(8,128)S(1)} %collective-permute-done.23.refs_2_, f32[128,1024]{1,0:T(8,128)S(1)} %collective-permute-done.24.refs_3_), custom_call_target="tpu_custom_call" | custom-call | bytes 2097152 | tf_op jit(solution)/shard_map/pallas_call | solution.py:50
  126.6 1.9 %shard_map.152 = (f32[1024,512]{1,0:T(8,128)}, f32[1024,512]{1,0:T(8,128)}) custom-call(s32[5]{0:T(128)S(1)} %stack.23.s, f32[128,1024]{1,0:T(8,128)S(1)} %add.100.refs_0_, f32[128,1024]{1,0:T(8,128)S(1)} %add.102.refs_1_, f32[128,1024]{1,0:T(8,128)S(1)} %collective-permute-done.18.refs_2_, ...), custom_call_target="tpu_custom_call", output_to_operand_aliasing={{0}: (5, {}), {1}: (6, {})} | custom-call | bytes 6291456 | tf_op jit(solution)/shard_map/pallas_call | solution.py:50
  (83 shorter events, 1.9 us)
Async XLA Ops:
  0.8 12.3 %copy-start.1 = (bf16[1024,512]{1,0:T(8,128)(2,1)S(1)}, bf16[1024,512]{1,0:T(8,128)(2,1)}, u32[]{:S(2)}) copy-start(bf16[1024,512]{1,0:T(8,128)(2,1)} %r1_ref.7) | copy-start | bytes 3145732
  0.8 12.3 %copy-start.2 = (bf16[1024,512]{1,0:T(8,128)(2,1)S(1)}, bf16[1024,512]{1,0:T(8,128)(2,1)}, u32[]{:S(2)}) copy-start(bf16[1024,512]{1,0:T(8,128)(2,1)} %r0_ref.7) | copy-start | bytes 3145732
  0.8 12.3 %copy-start.3 = (f32[512,512]{1,0:T(8,128)S(1)}, f32[512,512]{1,0:T(8,128)}, u32[]{:S(2)}) copy-start(f32[512,512]{1,0:T(8,128)} %inv1_ref.3) | copy-start | bytes 3145732
  0.8 12.3 %copy-start.4 = (f32[512,512]{1,0:T(8,128)S(1)}, f32[512,512]{1,0:T(8,128)}, u32[]{:S(2)}) copy-start(f32[512,512]{1,0:T(8,128)} %cross_ref.3) | copy-start | bytes 3145732
  0.8 12.3 %copy-start.5 = (f32[512,512]{1,0:T(8,128)S(1)}, f32[512,512]{1,0:T(8,128)}, u32[]{:S(2)}) copy-start(f32[512,512]{1,0:T(8,128)} %inv0_ref.3) | copy-start | bytes 3145732
  0.8 12.3 %copy-start.6 = (bf16[128,512]{1,0:T(8,128)(2,1)S(1)}, bf16[128,512]{1,0:T(8,128)(2,1)}, u32[]{:S(2)}) copy-start(bf16[128,512]{1,0:T(8,128)(2,1)} %p1_ref.3) | copy-start | bytes 393220
  0.8 12.3 %copy-start.7 = (bf16[128,512]{1,0:T(8,128)(2,1)S(1)}, bf16[128,512]{1,0:T(8,128)(2,1)}, u32[]{:S(2)}) copy-start(bf16[128,512]{1,0:T(8,128)(2,1)} %p0_ref.3) | copy-start | bytes 393220
  6.0 18.2 %collective-permute-start.3 = (f32[512,128]{1,0:T(8,128)S(1)}, f32[512,128]{1,0:T(8,128)S(1)}, u32[]{:S(2)}, u32[]{:S(2)}) collective-permute-start(f32[512,128]{1,0:T(8,128)S(1)} %get-tuple-element.45.refs_1_), channel_id=1, source_target_pairs={{0,1},{1,0},{2,3},{3,2},{4,5},{5,4},{6,7},{7,6},{8,9},{9,8},{10,11... | collective-permute-start | bytes 786440 | tf_op jit(solution)/shard_map/ppermute | solution.py:251
  9.0 15.3 %collective-permute-start.9 = (f32[512,128]{1,0:T(8,128)S(1)}, f32[512,128]{1,0:T(8,128)S(1)}, u32[]{:S(2)}, u32[]{:S(2)}) collective-permute-start(f32[512,128]{1,0:T(8,128)S(1)} %get-tuple-element.51.refs_3_), channel_id=1, source_target_pairs={{0,1},{1,0},{2,3},{3,2},{4,5},{5,4},{6,7},{7,6},{8,9},{9,8},{10,11... | collective-permute-start | bytes 786440 | tf_op jit(solution)/shard_map/ppermute | solution.py:251
  9.1 18.3 %collective-permute-start.12 = (f32[512,128]{1,0:T(8,128)S(1)}, f32[512,128]{1,0:T(8,128)S(1)}, u32[]{:S(2)}, u32[]{:S(2)}) collective-permute-start(f32[512,128]{1,0:T(8,128)S(1)} %get-tuple-element.53.refs_4_), channel_id=1, source_target_pairs={{0,1},{1,0},{2,3},{3,2},{4,5},{5,4},{6,7},{7,6},{8,9},{9,8},{10,11... | collective-permute-start | bytes 786440 | tf_op jit(solution)/shard_map/ppermute | solution.py:251
  11.1 33.6 %collective-permute-start.6 = (f32[512,256]{1,0:T(8,128)S(1)}, f32[512,256]{1,0:T(8,128)S(1)}, u32[]{:S(2)}, u32[]{:S(2)}) collective-permute-start(f32[512,256]{1,0:T(8,128)S(1)} %get-tuple-element.49.refs_2_), channel_id=1, source_target_pairs={{0,1},{1,0},{2,3},{3,2},{4,5},{5,4},{6,7},{7,6},{8,9},{9,8},{10,11... | collective-permute-start | bytes 1572872 | tf_op jit(solution)/shard_map/ppermute | solution.py:251
  11.1 66.6 %collective-permute-start = (f32[512,384]{1,0:T(8,128)S(1)}, f32[512,384]{1,0:T(8,128)S(1)}, u32[]{:S(2)}, u32[]{:S(2)}) collective-permute-start(f32[512,384]{1,0:T(8,128)S(1)} %get-tuple-element.39.refs_0_), channel_id=1, source_target_pairs={{0,1},{1,0},{2,3},{3,2},{4,5},{5,4},{6,7},{7,6},{8,9},{9,8},{10,11... | collective-permute-start | bytes 2359304 | tf_op jit(solution)/shard_map/ppermute | solution.py:251
  13.1 6.6 %copy-start = (bf16[1024,1024]{1,0:T(8,128)(2,1)S(1)}, bf16[1024,1024]{1,0:T(8,128)(2,1)}, u32[]{:S(2)}) copy-start(bf16[1024,1024]{1,0:T(8,128)(2,1)} %a_ref.5) | copy-start | bytes 6291460
  24.1 7.7 %collective-permute-start.25 = (f32[1056,128]{1,0:T(8,128)S(1)}, f32[1056,128]{1,0:T(8,128)S(1)}, u32[]{:S(2)}, u32[]{:S(2)}) collective-permute-start(f32[1056,128]{1,0:T(8,128)S(1)} %get-tuple-element.63), channel_id=1, source_target_pairs={{0,8},{8,0},{16,24},{24,16},{1,9},{9,1},{17,25},{25,17},{2,10},{10... | collective-permute-start | bytes 1622024 | tf_op jit(solution)/shard_map/ppermute | solution.py:251
  24.3 6.0 %collective-permute-start.4 = (f32[256,128]{1,0:T(8,128)S(1)}, f32[256,128]{1,0:T(8,128)S(1)}, u32[]{:S(2)}, u32[]{:S(2)}) collective-permute-start(f32[256,128]{1,0:T(8,128)S(1)} %bitcast.85), channel_id=1, source_target_pairs={{0,2},{1,3},{2,0},{3,1},{4,6},{5,7},{6,4},{7,5},{8,10},{9,11},{10,... | collective-permute-start | bytes 393224 | tf_op jit(solution)/shard_map/ppermute | solution.py:251
  27.4 33.1 %collective-permute-start.20 = (f32[128,1024]{1,0:T(8,128)S(1)}, f32[128,1024]{1,0:T(8,128)S(1)}, u32[]{:S(2)}, u32[]{:S(2)}) collective-permute-start(f32[128,1024]{1,0:T(8,128)S(1)} %shard_map.150), channel_id=1, source_target_pairs={{0,8},{8,0},{16,24},{24,16},{1,9},{9,1},{17,25},{25,17},{2,10},{10... | collective-permute-start | bytes 1572872 | tf_op jit(solution)/shard_map/ppermute | solution.py:251
  30.3 6.4 %collective-permute-start.10 = (f32[256,128]{1,0:T(8,128)S(1)}, f32[256,128]{1,0:T(8,128)S(1)}, u32[]{:S(2)}, u32[]{:S(2)}) collective-permute-start(f32[256,128]{1,0:T(8,128)S(1)} %bitcast.83), channel_id=1, source_target_pairs={{0,2},{1,3},{2,0},{3,1},{4,6},{5,7},{6,4},{7,5},{8,10},{9,11},{10,... | collective-permute-start | bytes 393224 | tf_op jit(solution)/shard_map/ppermute | solution.py:251
  31.9 7.6 %collective-permute-start.13 = (f32[256,128]{1,0:T(8,128)S(1)}, f32[256,128]{1,0:T(8,128)S(1)}, u32[]{:S(2)}, u32[]{:S(2)}) collective-permute-start(f32[256,128]{1,0:T(8,128)S(1)} %bitcast.84), channel_id=1, source_target_pairs={{0,2},{1,3},{2,0},{3,1},{4,6},{5,7},{6,4},{7,5},{8,10},{9,11},{10,... | collective-permute-start | bytes 393224 | tf_op jit(solution)/shard_map/ppermute | solution.py:251
  36.6 7.3 %collective-permute-start.26 = (f32[528,128]{1,0:T(8,128)S(1)}, f32[528,128]{1,0:T(8,128)S(1)}, u32[]{:S(2)}, u32[]{:S(2)}) collective-permute-start(f32[528,128]{1,0:T(8,128)S(1)} %dynamic-slice_bitcast_fusion), channel_id=1, source_target_pairs={{0,2},{1,3},{2,0},{3,1},{4,6},{5,7},{6,4},{7,5},{8,10},{9,11},{10,... | collective-permute-start | bytes 811016 | tf_op jit(solution)/shard_map/ppermute | solution.py:251
  39.4 44.8 %collective-permute-start.15 = (f32[384,1024]{1,0:T(8,128)S(1)}, f32[384,1024]{1,0:T(8,128)S(1)}, u32[]{:S(2)}, u32[]{:S(2)}) collective-permute-start(f32[384,1024]{1,0:T(8,128)S(1)} %get-tuple-element.55), channel_id=1, source_target_pairs={{0,8},{8,0},{16,24},{24,16},{1,9},{9,1},{17,25},{25,17},{2,10},{10... | collective-permute-start | bytes 4718600 | tf_op jit(solution)/shard_map/ppermute | solution.py:251
  44.0 13.6 %collective-permute-start.27 = (f32[264,128]{1,0:T(8,128)S(1)}, f32[264,128]{1,0:T(8,128)S(1)}, u32[]{:S(2)}, u32[]{:S(2)}) collective-permute-start(f32[264,128]{1,0:T(8,128)S(1)} %dynamic-slice_bitcast_fusion.3), channel_id=1, source_target_pairs={{0,1},{1,0},{2,3},{3,2},{4,5},{5,4},{6,7},{7,6},{8,9},{9,8},{10,11... | collective-permute-start | bytes 405512 | tf_op jit(solution)/shard_map/ppermute | solution.py:251
  44.8 22.9 %collective-permute-start.7 = (f32[256,256]{1,0:T(8,128)S(1)}, f32[256,256]{1,0:T(8,128)S(1)}, u32[]{:S(2)}, u32[]{:S(2)}) collective-permute-start(f32[256,256]{1,0:T(8,128)S(1)} %bitcast.82), channel_id=1, source_target_pairs={{0,2},{1,3},{2,0},{3,1},{4,6},{5,7},{6,4},{7,5},{8,10},{9,11},{10,... | collective-permute-start | bytes 786440 | tf_op jit(solution)/shard_map/ppermute | solution.py:251
  57.6 8.6 %collective-permute-start.28 = (f32[264,128]{1,0:T(8,128)S(1)}, f32[264,128]{1,0:T(8,128)S(1)}, u32[]{:S(2)}, u32[]{:S(2)}) collective-permute-start(f32[264,128]{1,0:T(8,128)S(1)} %bitcast_add_fusion.3), channel_id=1, source_target_pairs={{0,4},{1,5},{2,6},{3,7},{4,0},{5,1},{6,2},{7,3},{8,12},{9,13},{10,... | collective-permute-start | bytes 405512 | tf_op jit(solution)/shard_map/ppermute | solution.py:251
  60.6 38.5 %collective-permute-start.21 = (f32[128,1024]{1,0:T(8,128)S(1)}, f32[128,1024]{1,0:T(8,128)S(1)}, u32[]{:S(2)}, u32[]{:S(2)}) collective-permute-start(f32[128,1024]{1,0:T(8,128)S(1)} %add.103), channel_id=1, source_target_pairs={{0,16},{8,24},{16,0},{24,8},{1,17},{9,25},{17,1},{25,9},{2,18},{10... | collective-permute-start | bytes 1572872 | tf_op jit(solution)/shard_map/ppermute | solution.py:251
  66.2 9.9 %collective-permute-start.29 = (f32[264,128]{1,0:T(8,128)S(1)}, f32[264,128]{1,0:T(8,128)S(1)}, u32[]{:S(2)}, u32[]{:S(2)}) collective-permute-start(f32[264,128]{1,0:T(8,128)S(1)} %add.110), channel_id=1, source_target_pairs={{0,16},{8,24},{16,0},{24,8},{1,17},{9,25},{17,1},{25,9},{2,18},{10... | collective-permute-start | bytes 405512 | tf_op jit(solution)/shard_map/ppermute | solution.py:251
  76.1 6.5 %collective-permute-start.30 = (f32[264,128]{1,0:T(8,128)S(1)}, f32[264,128]{1,0:T(8,128)S(1)}, u32[]{:S(2)}, u32[]{:S(2)}) collective-permute-start(f32[264,128]{1,0:T(8,128)S(1)} %add.111), channel_id=1, source_target_pairs={{0,2},{1,3},{2,0},{3,1},{4,6},{5,7},{6,4},{7,5},{8,10},{9,11},{10,... | collective-permute-start | bytes 405512 | tf_op jit(solution)/shard_map/ppermute | solution.py:251
  77.9 10.1 %collective-permute-start.1 = (f32[256,384]{1,0:T(8,128)S(1)}, f32[256,384]{1,0:T(8,128)S(1)}, u32[]{:S(2)}, u32[]{:S(2)}) collective-permute-start(f32[256,384]{1,0:T(8,128)S(1)} %bitcast.81), channel_id=1, source_target_pairs={{0,2},{1,3},{2,0},{3,1},{4,6},{5,7},{6,4},{7,5},{8,10},{9,11},{10,... | collective-permute-start | bytes 1179656 | tf_op jit(solution)/shard_map/ppermute | solution.py:251
  82.7 7.0 %collective-permute-start.31 = (f32[528,128]{1,0:T(8,128)S(1)}, f32[528,128]{1,0:T(8,128)S(1)}, u32[]{:S(2)}, u32[]{:S(2)}) collective-permute-start(f32[528,128]{1,0:T(8,128)S(1)} %pad_maximum_fusion.1), channel_id=1, source_target_pairs={{0,1},{1,0},{2,3},{3,2},{4,5},{5,4},{6,7},{7,6},{8,9},{9,8},{10,11... | collective-permute-start | bytes 811016 | tf_op jit(solution)/shard_map/ppermute | solution.py:251
  84.5 17.5 %collective-permute-start.22 = (f32[128,1024]{1,0:T(8,128)S(1)}, f32[128,1024]{1,0:T(8,128)S(1)}, u32[]{:S(2)}, u32[]{:S(2)}) collective-permute-start(f32[128,1024]{1,0:T(8,128)S(1)} %get-tuple-element.68), channel_id=1, source_target_pairs={{0,16},{8,24},{16,0},{24,8},{1,17},{9,25},{17,1},{25,9},{2,18},{10... | collective-permute-start | bytes 1572872 | tf_op jit(solution)/shard_map/ppermute | solution.py:251
  86.1 24.1 %collective-permute-start.17 = (f32[128,1024]{1,0:T(8,128)S(1)}, f32[128,1024]{1,0:T(8,128)S(1)}, u32[]{:S(2)}, u32[]{:S(2)}) collective-permute-start(f32[128,1024]{1,0:T(8,128)S(1)} %get-tuple-element.69), channel_id=1, source_target_pairs={{0,16},{8,24},{16,0},{24,8},{1,17},{9,25},{17,1},{25,9},{2,18},{10... | collective-permute-start | bytes 1572872 | tf_op jit(solution)/shard_map/ppermute | solution.py:251
  88.1 27.8 %collective-permute-start.16 = (f32[128,1024]{1,0:T(8,128)S(1)}, f32[128,1024]{1,0:T(8,128)S(1)}, u32[]{:S(2)}, u32[]{:S(2)}) collective-permute-start(f32[128,1024]{1,0:T(8,128)S(1)} %get-tuple-element.70), channel_id=1, source_target_pairs={{0,16},{8,24},{16,0},{24,8},{1,17},{9,25},{17,1},{25,9},{2,18},{10... | collective-permute-start | bytes 1572872 | tf_op jit(solution)/shard_map/ppermute | solution.py:251
  89.6 9.4 %collective-permute-start.5 = (f32[128,128]{1,0:T(8,128)S(1)}, f32[128,128]{1,0:T(8,128)S(1)}, u32[]{:S(2)}, u32[]{:S(2)}) collective-permute-start(f32[128,128]{1,0:T(8,128)S(1)} %get-tuple-element.93), channel_id=1, source_target_pairs={{0,4},{1,5},{2,6},{3,7},{4,0},{5,1},{6,2},{7,3},{8,12},{9,13},{10,... | collective-permute-start | bytes 196616 | tf_op jit(solution)/shard_map/ppermute | solution.py:251
  99.1 17.0 %collective-permute-start.11 = (f32[128,128]{1,0:T(8,128)S(1)}, f32[128,128]{1,0:T(8,128)S(1)}, u32[]{:S(2)}, u32[]{:S(2)}) collective-permute-start(f32[128,128]{1,0:T(8,128)S(1)} %get-tuple-element.91), channel_id=1, source_target_pairs={{0,4},{1,5},{2,6},{3,7},{4,0},{5,1},{6,2},{7,3},{8,12},{9,13},{10,... | collective-permute-start | bytes 196616 | tf_op jit(solution)/shard_map/ppermute | solution.py:251
  99.1 17.6 %collective-permute-start.14 = (f32[128,128]{1,0:T(8,128)S(1)}, f32[128,128]{1,0:T(8,128)S(1)}, u32[]{:S(2)}, u32[]{:S(2)}) collective-permute-start(f32[128,128]{1,0:T(8,128)S(1)} %get-tuple-element.89), channel_id=1, source_target_pairs={{0,4},{1,5},{2,6},{3,7},{4,0},{5,1},{6,2},{7,3},{8,12},{9,13},{10,... | collective-permute-start | bytes 196616 | tf_op jit(solution)/shard_map/ppermute | solution.py:251
  102.0 14.8 %collective-permute-start.8 = (f32[128,256]{1,0:T(8,128)S(1)}, f32[128,256]{1,0:T(8,128)S(1)}, u32[]{:S(2)}, u32[]{:S(2)}) collective-permute-start(f32[128,256]{1,0:T(8,128)S(1)} %get-tuple-element.85), channel_id=1, source_target_pairs={{0,4},{1,5},{2,6},{3,7},{4,0},{5,1},{6,2},{7,3},{8,12},{9,13},{10,... | collective-permute-start | bytes 393224 | tf_op jit(solution)/shard_map/ppermute | solution.py:251
  110.2 8.7 %collective-permute-start.2 = (f32[128,384]{1,0:T(8,128)S(1)}, f32[128,384]{1,0:T(8,128)S(1)}, u32[]{:S(2)}, u32[]{:S(2)}) collective-permute-start(f32[128,384]{1,0:T(8,128)S(1)} %get-tuple-element.77), channel_id=1, source_target_pairs={{0,4},{1,5},{2,6},{3,7},{4,0},{5,1},{6,2},{7,3},{8,12},{9,13},{10,... | collective-permute-start | bytes 589832 | tf_op jit(solution)/shard_map/ppermute | solution.py:251
  115.8 6.6 %collective-permute-start.32 = (f32[1056,128]{1,0:T(8,128)S(1)}, f32[1056,128]{1,0:T(8,128)S(1)}, u32[]{:S(2)}, u32[]{:S(2)}) collective-permute-start(f32[1056,128]{1,0:T(8,128)S(1)} %bitcast.64), channel_id=1, source_target_pairs={{0,8},{8,0},{16,24},{24,16},{1,9},{9,1},{17,25},{25,17},{2,10},{10... | collective-permute-start | bytes 1622024 | tf_op jit(solution)/shard_map/ppermute | solution.py:251
  116.1 8.5 %collective-permute-start.23 = (f32[128,1024]{1,0:T(8,128)S(1)}, f32[128,1024]{1,0:T(8,128)S(1)}, u32[]{:S(2)}, u32[]{:S(2)}) collective-permute-start(f32[128,1024]{1,0:T(8,128)S(1)} %add.104.refs_0_), channel_id=1, source_target_pairs={{0,8},{8,0},{16,24},{24,16},{1,9},{9,1},{17,25},{25,17},{2,10},{10... | collective-permute-start | bytes 1572872 | tf_op jit(solution)/shard_map/ppermute | solution.py:251
  116.7 8.0 %collective-permute-start.24 = (f32[128,1024]{1,0:T(8,128)S(1)}, f32[128,1024]{1,0:T(8,128)S(1)}, u32[]{:S(2)}, u32[]{:S(2)}) collective-permute-start(f32[128,1024]{1,0:T(8,128)S(1)} %add.106.refs_1_), channel_id=1, source_target_pairs={{0,8},{8,0},{16,24},{24,16},{1,9},{9,1},{17,25},{25,17},{2,10},{10... | collective-permute-start | bytes 1572872 | tf_op jit(solution)/shard_map/ppermute | solution.py:251
  116.8 9.8 %collective-permute-start.19 = (f32[128,1024]{1,0:T(8,128)S(1)}, f32[128,1024]{1,0:T(8,128)S(1)}, u32[]{:S(2)}, u32[]{:S(2)}) collective-permute-start(f32[128,1024]{1,0:T(8,128)S(1)} %add.102.refs_1_), channel_id=1, source_target_pairs={{0,8},{8,0},{16,24},{24,16},{1,9},{9,1},{17,25},{25,17},{2,10},{10... | collective-permute-start | bytes 1572872 | tf_op jit(solution)/shard_map/ppermute | solution.py:251
  118.9 7.7 %collective-permute-start.18 = (f32[128,1024]{1,0:T(8,128)S(1)}, f32[128,1024]{1,0:T(8,128)S(1)}, u32[]{:S(2)}, u32[]{:S(2)}) collective-permute-start(f32[128,1024]{1,0:T(8,128)S(1)} %add.100.refs_0_), channel_id=1, source_target_pairs={{0,8},{8,0},{16,24},{24,16},{1,9},{9,1},{17,25},{25,17},{2,10},{10... | collective-permute-start | bytes 1572872 | tf_op jit(solution)/shard_map/ppermute | solution.py:251
